TPU v7x, 768 devices: a whole 4x8x12 slice. The times are simulated.
768 devices in a mesh: dom: 96 (over x, z, core), sub: 8 (over y).
Axes of the slice: x: 4, y: 8, z: 12, core: 2. Of those that a mesh axis runs over, the one named last changes fastest.
Arguments:
- adjoint_field: float32 [98304, 5, 512], P(('dom', 'sub')), may hold values from -6 to 6
- metric: float32 [98304, 3, 512], P(('dom', 'sub')), may hold values from 0.5 to 4
- velocity: float32 [98304, 3, 512], P(('dom', 'sub')), may hold values from -2 to 2
- mortar_route: int32 [98304, 1], P(('dom', 'sub')), may hold values from 0 to 95, as said below
- mortar_element: int32 [98304, 1], P(('dom', 'sub')), may hold values from 0 to 127
- face_code: int32 [98304, 1], P(('dom', 'sub')), may hold values from 0 to 7
- hanging: int32 [98304, 1], P(('dom', 'sub')), may hold values 0 or 1
Outputs:
- result: float32 [98304, 5, 512], P(('dom', 'sub'))
Inputs may be any that keep to these rules, and one draw needn't show every extreme that they name: `mortar_route`: each element's value is its own device's dom index d or one of d - 2, d - 1, d + 1, d + 2 taken modulo 96. In each aligned block of 128 rows (the elements of one device) no value is named by more than 96 rows, and some value by exactly 96.
All inputs are finite; a program needn't handle non-finite values. No bound on the sum of `hanging` on one device may be relied on, other than what follows from the above.
Results may differ from a plain program's by a relative error of at most 0.00088.
Values may be sent and summed in bfloat16 or wider, within the bound.
A program may use at most 32 MiB of HBM per device.

v0:
```python
import jax
import jax.numpy as jnp
import numpy as np
from jax import lax
from jax.sharding import PartitionSpec as P

gll_nodes = np.array(
    [
        -1.0,
        -0.8717401485096066,
        -0.5917001814331423,
        -0.2092992179024789,
        0.2092992179024789,
        0.5917001814331423,
        0.8717401485096066,
        1.0,
    ]
)
viscosity = 0.005


def passed_along(block, axis, distance):
    devices = range(lax.axis_size(axis))
    route = [((i - distance) % len(devices), i) for i in devices]
    return lax.ppermute(block, axis, route)


def extended(block, sides, width):
    for axis, dim in sides:
        count = lax.axis_size(axis)
        forward = [(i, i + 1) for i in range(count - 1)]
        backward = [(target, source) for source, target in forward]
        low = lax.ppermute(
            lax.slice_in_dim(block, block.shape[dim] - width, None, axis=dim), axis, forward
        )
        high = lax.ppermute(lax.slice_in_dim(block, 0, width, axis=dim), axis, backward)
        block = jnp.concatenate([low, block, high], axis=dim)
    return block


def legendre_seven(points):
    prev = np.ones(points.shape)
    curr = np.array(points)
    for order in range(1, 7):
        nxt = ((2 * order + 1) * points * curr - order * prev) / (order + 1)
        prev, curr = (curr, nxt)
    return curr


def diff_matrix():
    values = legendre_seven(gll_nodes)
    result_mat = np.zeros((8, 8))
    for row in range(8):
        for col in range(8):
            if row != col:
                result_mat[row, col] = values[row] / (
                    values[col] * (gll_nodes[row] - gll_nodes[col])
                )
    result_mat[0, 0] = -14.0
    result_mat[7, 7] = 14.0
    return result_mat


def lagrange_at(points):
    basis = np.ones((8, 8))
    for row in range(8):
        for col in range(8):
            for other in range(8):
                if other != col:
                    basis[row, col] *= (points[row] - gll_nodes[other]) / (
                        gll_nodes[col] - gll_nodes[other]
                    )
    return basis


def face_tables():
    halves = [lagrange_at((gll_nodes - 1.0) / 2.0), lagrange_at((gll_nodes + 1.0) / 2.0)]
    perm_mat = np.zeros((64, 64))
    for col in range(64):
        perm_mat[col % 8 * 8 + col // 8, col] = 1.0
    tables = []
    for code in range(8):
        mat = np.kron(halves[code % 2], halves[code // 2 % 2])
        if code >= 4:
            mat = mat @ perm_mat
        tables.append(mat)
    return np.stack(tables).astype(np.float32)


def kron_tables():
    dmat = diff_matrix()
    eye_eight = np.eye(8)
    first = np.kron(np.kron(eye_eight, dmat), eye_eight)
    second = np.kron(np.kron(eye_eight, eye_eight), dmat)
    return (dmat.astype(np.float32), first.astype(np.float32), second.astype(np.float32))


def fold_faces(fine, codes):
    tables = jnp.asarray(face_tables())
    total = jnp.zeros(fine.shape, jnp.float32)
    for code in range(8):
        mapped = jnp.einsum("efa,ab->efb", fine, tables[code], precision=lax.Precision.HIGHEST)
        total = total + jnp.where((codes == code)[:, :, None], mapped, 0.0)
    return total


def derive(field, dim, mats):
    dmat, first, second = mats
    count = field.shape[0]
    if dim == 0:
        cube = field.reshape(count, 5, 8, 64)
        return jnp.einsum("ai,efip->efap", dmat, cube, precision=lax.Precision.HIGHEST).reshape(
            count, 5, 512
        )
    kron_mat = first if dim == 1 else second
    return jnp.einsum("efp,qp->efq", field, kron_mat, precision=lax.Precision.HIGHEST)


def derive_back(field, dim, mats):
    dmat, first, second = mats
    count = field.shape[0]
    if dim == 0:
        cube = field.reshape(count, 5, 8, 64)
        return jnp.einsum("ai,efap->efip", dmat, cube, precision=lax.Precision.HIGHEST).reshape(
            count, 5, 512
        )
    kron_mat = first if dim == 1 else second
    return jnp.einsum("efq,qp->efp", field, kron_mat, precision=lax.Precision.HIGHEST)


def apply_adjoint(summed, metric, velocity):
    mats = tuple((jnp.asarray(m) for m in kron_tables()))
    total = jnp.zeros(summed.shape, jnp.float32)
    for dim in range(3):
        inner = (
            viscosity * metric[:, dim : dim + 1] * derive(summed, dim, mats)
            + velocity[:, dim : dim + 1] * summed
        )
        total = total + derive_back(inner, dim, mats)
    return total


def shards(adjoint_field, metric, velocity, mortar_route, mortar_element, face_code, hanging):
    elems = adjoint_field.shape[0]
    field_cube = adjoint_field.reshape(elems, 5, 8, 8, 8)
    fine = field_cube[:, :, :, 7, :].reshape(elems, 5, 64)
    hang_f = hanging.astype(jnp.float32)
    folded = (
        (fold_faces(fine, face_code) * hang_f[:, :, None]).astype(jnp.bfloat16).reshape(elems, 320)
    )
    local_ids = jnp.arange(elems, dtype=jnp.int32)
    peers = lax.axis_size("dom")
    cap = max(2, 3 * elems // 4)
    offset_slot = (mortar_route[:, 0] - lax.axis_index("dom") + 2 + peers) % peers
    onehot = (offset_slot[:, None] == jnp.arange(5, dtype=jnp.int32)[None, :]).astype(jnp.int32)
    rank = jnp.sum(jnp.cumsum(onehot, axis=0) * onehot, axis=1) - 1
    slot = offset_slot * cap + rank
    select_int = (slot[None, :] == jnp.arange(5 * cap, dtype=jnp.int32)[:, None]).astype(jnp.int32)
    send_faces = (
        jnp.dot(select_int.astype(jnp.bfloat16), folded, preferred_element_type=jnp.float32)
        .astype(jnp.bfloat16)
        .reshape(5, cap, 320)
    )
    send_dest = (jnp.sum(select_int * (mortar_element[:, 0] + 1)[None, :], axis=1) - 1).reshape(
        5, cap
    )

    def absorb(total, faces, dest):
        hit = (dest[None, :] == local_ids[:, None]).astype(jnp.bfloat16)
        return total + jnp.dot(hit, faces, preferred_element_type=jnp.float32)

    mortar = absorb(jnp.zeros((elems, 320), jnp.float32), send_faces[2], send_dest[2])
    for position, offset in ((0, -2), (1, -1), (3, 1), (4, 2)):
        got_faces, got_dest = passed_along(
            (send_faces[position], send_dest[position]), "dom", offset
        )
        mortar = absorb(mortar, got_faces, got_dest)
    keep = (1.0 - hang_f)[:, :, None, None]
    field_cube = field_cube.at[:, :, :, 7, :].set(field_cube[:, :, :, 7, :] * keep)
    field_cube = field_cube.at[:, :, :, 0, :].add(mortar.reshape(elems, 5, 8, 8))
    high_faces = field_cube[:, :, 7]
    low_faces = field_cube[:, :, 0]
    edges = jnp.stack([low_faces[0], high_faces[-1]])
    padded = extended(edges, ((("dom", "sub"), 0),), 1)
    shared = high_faces[:-1] + low_faces[1:]
    new_high = jnp.concatenate([shared, high_faces[-1:] + padded[3:4]], axis=0)
    new_low = jnp.concatenate([low_faces[:1] + padded[0:1], shared], axis=0)
    field_cube = field_cube.at[:, :, 7].set(new_high).at[:, :, 0].set(new_low)
    return apply_adjoint(field_cube.reshape(elems, 5, 512), metric, velocity)


def solution(mesh):
    return jax.shard_map(
        shards,
        mesh=mesh,
        in_specs=(
            P(("dom", "sub"), None, None),
            P(("dom", "sub"), None, None),
            P(("dom", "sub"), None, None),
            P(("dom", "sub"), None),
            P(("dom", "sub"), None),
            P(("dom", "sub"), None),
            P(("dom", "sub"), None),
        ),
        out_specs=P(("dom", "sub"), None, None),
        check_vma=False,
    )
```

profile of v0, /device:TPU:24, one launch (start us, length us, event | category | flops | bytes accessed | tf_op | source)
XLA Modules:
  0.0 102.1 jit_solution(8424818099867504191)
XLA Ops:
  0.7 0.7 fusion.49
  1.8 0.7 fusion.48
  3.2 16.2 %collective-permute-start.2 = (s32[96]{0:T(128)}, s32[96]{0:T(128)}, u32[]{:S(2)}, u32[]{:S(2)}) collective-permute-start(s32[96]{0:T(128)} %get-tuple-element.67), channel_id=1, source_target_pairs={{8,0},{16,8},{24,16},{32,24},{40,32},{48,40},{56,48},{64,56},{72,6... | collective-permute-start | bytes 1160 | tf_op jit(solution)/shard_map/ppermute | solution.py:25
  19.4 1.9 %collective-permute-start.6 = (s32[96]{0:T(128)}, s32[96]{0:T(128)}, u32[]{:S(2)}, u32[]{:S(2)}) collective-permute-start(s32[96]{0:T(128)} %get-tuple-element.68), channel_id=1, source_target_pairs={{752,0},{760,8},{0,16},{8,24},{16,32},{24,40},{32,48},{40,56},{48,... | collective-permute-start | bytes 1160 | tf_op jit(solution)/shard_map/ppermute | solution.py:25
  21.4 1.9 %collective-permute-start.4 = (s32[96]{0:T(128)}, s32[96]{0:T(128)}, u32[]{:S(2)}, u32[]{:S(2)}) collective-permute-start(s32[96]{0:T(128)} %get-tuple-element.69), channel_id=1, source_target_pairs={{760,0},{0,8},{8,16},{16,24},{24,32},{32,40},{40,48},{48,56},{56,6... | collective-permute-start | bytes 1160 | tf_op jit(solution)/shard_map/ppermute | solution.py:25
  23.3 7.2 %collective-permute-start = (s32[96]{0:T(128)}, s32[96]{0:T(128)}, u32[]{:S(2)}, u32[]{:S(2)}) collective-permute-start(s32[96]{0:T(128)} %get-tuple-element.70), channel_id=1, source_target_pairs={{16,0},{24,8},{32,16},{40,24},{48,32},{56,40},{64,48},{72,56},{80,... | collective-permute-start | bytes 1160 | tf_op jit(solution)/shard_map/ppermute | solution.py:25
  31.2 0.7 compare_bitcast_fusion
  31.9 1.7 %copy.47 = f32[128,5,512]{0,2,1:T(8,128)S(1)} copy(f32[128,5,512]{2,0,1:T(8,128)} %param.19) | data formatting | bytes 2621440 | tf_op args[0]
  36.6 1.9 %collective-permute-start.1 = (bf16[96,320]{0,1:T(8,128)(2,1)S(1)}, bf16[96,320]{0,1:T(8,128)(2,1)S(1)}, u32[]{:S(2)}, u32[]{:S(2)}) collective-permute-start(bf16[96,320]{0,1:T(8,128)(2,1)S(1)} %get-tuple-element.66), channel_id=1, source_target_pairs={{16,0},{24,8},{32,16},{40,24},{48,32},{56,40},{64,48},{72,56},{80,... | collective-permute-start | bytes 184328 | tf_op jit(solution)/shard_map/ppermute | solution.py:25
  39.1 2.0 %slice_bitcast_fusion = (f32[128,512]{1,0:T(8,128)}, f32[128,1,512]{2,0,1:T(8,128)S(1)}, f32[128,512]{1,0:T(8,128)}) fusion(f32[128,3,512]{2,0,1:T(8,128)} %param.21), kind=kLoop, calls=%fused_computation.32 | loop fusion | bytes 1572864 | tf_op jit(solution)/shard_map/mul | solution.py:137
  41.5 0.8 copy.62
  42.8 3.4 %collective-permute-start.3 = (bf16[96,320]{0,1:T(8,128)(2,1)S(1)}, bf16[96,320]{0,1:T(8,128)(2,1)S(1)}, u32[]{:S(2)}, u32[]{:S(2)}) collective-permute-start(bf16[96,320]{0,1:T(8,128)(2,1)S(1)} %get-tuple-element.63), channel_id=1, source_target_pairs={{8,0},{16,8},{24,16},{32,24},{40,32},{48,40},{56,48},{64,56},{72,6... | collective-permute-start | bytes 184328 | tf_op jit(solution)/shard_map/ppermute | solution.py:25
  46.2 3.6 %collective-permute-start.7 = (bf16[96,320]{0,1:T(8,128)(2,1)S(1)}, bf16[96,320]{0,1:T(8,128)(2,1)S(1)}, u32[]{:S(2)}, u32[]{:S(2)}) collective-permute-start(bf16[96,320]{0,1:T(8,128)(2,1)S(1)} %get-tuple-element.64), channel_id=1, source_target_pairs={{752,0},{760,8},{0,16},{8,24},{16,32},{24,40},{32,48},{40,56},{48,... | collective-permute-start | bytes 184328 | tf_op jit(solution)/shard_map/ppermute | solution.py:25
  49.8 0.9 convolution_add_fusion.3
  50.7 1.9 %collective-permute-start.5 = (bf16[96,320]{0,1:T(8,128)(2,1)S(1)}, bf16[96,320]{0,1:T(8,128)(2,1)S(1)}, u32[]{:S(2)}, u32[]{:S(2)}) collective-permute-start(bf16[96,320]{0,1:T(8,128)(2,1)S(1)} %get-tuple-element.65), channel_id=1, source_target_pairs={{760,0},{0,8},{8,16},{16,24},{24,32},{32,40},{40,48},{48,56},{56,6... | collective-permute-start | bytes 184328 | tf_op jit(solution)/shard_map/ppermute | solution.py:25
  52.6 3.2 %collective-permute-done.7 = bf16[96,320]{0,1:T(8,128)(2,1)S(1)} collective-permute-done((bf16[96,320]{0,1:T(8,128)(2,1)S(1)}, bf16[96,320]{0,1:T(8,128)(2,1)S(1)}, u32[]{:S(2)}, u32[]{:S(2)}) %collective-permute-start.7) | collective-permute-done | bytes 61472 | tf_op jit(solution)/shard_map/ppermute | solution.py:25
  55.8 0.8 fusion.41
  56.7 3.1 %collective-permute-done.5 = bf16[96,320]{0,1:T(8,128)(2,1)S(1)} collective-permute-done((bf16[96,320]{0,1:T(8,128)(2,1)S(1)}, bf16[96,320]{0,1:T(8,128)(2,1)S(1)}, u32[]{:S(2)}, u32[]{:S(2)}) %collective-permute-start.5) | collective-permute-done | bytes 61472 | tf_op jit(solution)/shard_map/ppermute | solution.py:25
  59.8 0.8 fusion.40
  60.6 0.9 fusion.13
  61.6 4.7 %collective-permute-start.9 = (f32[1,5,8,8]{0,3,2,1:T(8,128)S(1)}, f32[1,5,8,8]{0,3,2,1:T(8,128)S(1)}, u32[]{:S(2)}, u32[]{:S(2)}) collective-permute-start(f32[1,5,8,8]{0,3,2,1:T(8,128)S(1)} %get-tuple-element.55), channel_id=1, source_target_pairs={{0,1},{1,2},{2,3},{3,4},{4,5},{5,6},{6,7},{7,8},{8,9},{9,10},{10,1... | collective-permute-start | bytes 3848 | tf_op jit(solution)/shard_map/ppermute | solution.py:33
  66.3 2.1 %collective-permute-start.8 = (f32[1,5,8,8]{0,3,2,1:T(8,128)S(1)}, f32[1,5,8,8]{0,3,2,1:T(8,128)S(1)}, u32[]{:S(2)}, u32[]{:S(2)}) collective-permute-start(f32[1,5,8,8]{0,3,2,1:T(8,128)S(1)} %get-tuple-element.56), channel_id=1, source_target_pairs={{1,0},{2,1},{3,2},{4,3},{5,4},{6,5},{7,6},{8,7},{9,8},{10,9},{11,1... | collective-permute-start | bytes 3848 | tf_op jit(solution)/shard_map/ppermute | solution.py:36
  69.1 5.6 %collective-permute-done.8 = f32[1,5,8,8]{0,3,2,1:T(8,128)S(1)} collective-permute-done((f32[1,5,8,8]{0,3,2,1:T(8,128)S(1)}, f32[1,5,8,8]{0,3,2,1:T(8,128)S(1)}, u32[]{:S(2)}, u32[]{:S(2)}) %collective-permute-start.8) | collective-permute-done | bytes 1312 | tf_op jit(solution)/shard_map/ppermute | solution.py:36
  75.1 1.8 %copy.56 = f32[128,5,8,8,8]{0,2,4,3,1:T(8,128)} copy(f32[128,5,8,8,8]{0,4,3,2,1:T(8,128)S(1)} %fusion.19) | data formatting | bytes 2621440 | tf_op jit(solution)/shard_map/scatter | solution.py:188
  77.6 3.1 %fusion.3 = f32[128,5,8,64]{0,2,3,1:T(8,128)S(1)} fusion(f32[128,5,8,64]{0,2,3,1:T(8,128)} %bitcast.154, f32[8,8,1,1]{1,0,3,2:T(8,128)S(1)} %copy-done.15, f32[128,8,64]{0,1,2:T(8,128)S(1)} %copy.58, f32[128,8,64]{0,1,2:T(8,128)S(1)} %copy.46), kind=kOutput, calls=%fused_computation.9 | convolution fusion | flops 32440320 | bytes 3145984 | tf_op jit(solution)/shard_map/ai,efip->efap/dot_general | solution.py:112
  80.7 1.2 %convolution_bitcast_fusion = f32[128,5,8,64]{0,2,3,1:T(8,128)S(1)} fusion(f32[128,5,8,64]{0,2,3,1:T(8,128)S(1)} %fusion.3, f32[8,8,1,1]{1,0,3,2:T(8,128)S(1)} %copy-done.15), kind=kOutput, calls=%fused_computation.6 | convolution fusion | flops 31457280 | bytes 2621696 | tf_op jit(solution)/shard_map/ai,efap->efip/dot_general | solution.py:124
  81.9 1.3 %copy.60 = f32[128,5,8,64]{0,3,2,1:T(8,128)} copy(f32[128,5,8,64]{0,2,3,1:T(8,128)S(1)} %convolution_bitcast_fusion) | data formatting | bytes 2621440 | tf_op jit(solution)/shard_map/ai,efap->efip/transpose | solution.py:124
  83.2 2.8 %copy.65 = f32[128,5,512]{2,0,1:T(8,128)} copy(f32[128,5,512]{0,2,1:T(8,128)} %bitcast.155) | data formatting | bytes 2621440 | tf_op jit(solution)/shard_map/reshape | solution.py:124
  86.1 5.7 %fusion.1 = f32[128,5,512]{2,0,1:T(8,128)S(1)} fusion(f32[128,5,512]{0,2,1:T(8,128)S(1)} %bitcast.152, f32[512,512,1]{1,0,2:T(8,128)} %constant.201, f32[128,5,512]{2,0,1:T(8,128)S(1)} %copy.64, f32[128,512]{1,0:T(8,128)S(1)} %copy-done.5, f32[128,512]{1,0:T(8,128)S(1)} %copy-done.3), kind=kOutput, calls=%fused_computation.5 | convolution fusion | flops 2014248960 | bytes 5505024 | tf_op jit(solution)/shard_map/efp,qp->efq/dot_general | solution.py:116
  91.9 2.2 %convolution_add_fusion.1 = f32[128,5,512]{2,0,1:T(8,128)S(1)} fusion(f32[128,5,512]{2,0,1:T(8,128)S(1)} %copy-done, f32[128,5,512]{2,0,1:T(8,128)S(1)} %fusion.1, f32[512,512,1]{1,0,2:T(8,128)S(1)} %copy-done.2), kind=kOutput, calls=%fused_computation.3 | convolution fusion | flops 2013593600 | bytes 4980736 | tf_op jit(solution)/shard_map/efq,qp->efp/dot_general | solution.py:128
  94.1 4.6 %fusion = f32[128,5,512]{2,0,1:T(8,128)S(1)} fusion(f32[128,5,512]{0,2,1:T(8,128)S(1)} %bitcast.153, f32[512,512,1]{1,0,2:T(8,128)S(1)} %copy-done.1, f32[128,5,512]{2,0,1:T(8,128)S(1)} %copy.64, f32[128,512]{1,0:T(8,128)S(1)} %copy-done.4, f32[128,512]{1,0:T(8,128)S(1)} %copy.67), kind=kOutput, calls=%fused_computation.2 | convolution fusion | flops 2014248960 | bytes 5505024 | tf_op jit(solution)/shard_map/efp,qp->efq/dot_general | solution.py:116
  98.7 3.3 %convolution_add_fusion = f32[128,5,512]{2,0,1:T(8,128)} fusion(f32[128,5,512]{2,0,1:T(8,128)S(1)} %convolution_add_fusion.1, f32[128,5,512]{2,0,1:T(8,128)S(1)} %fusion, f32[512,512,1]{1,0,2:T(8,128)S(1)} %copy-done.1), kind=kOutput, calls=%fused_computation | convolution fusion | flops 2013593600 | bytes 4980736 | tf_op jit(solution)/shard_map/efq,qp->efp/dot_general | solution.py:128
  (80 shorter events, 8.6 us)
Async XLA Ops:
  3.2 57.4 %collective-permute-start.2 = (s32[96]{0:T(128)}, s32[96]{0:T(128)}, u32[]{:S(2)}, u32[]{:S(2)}) collective-permute-start(s32[96]{0:T(128)} %get-tuple-element.67), channel_id=1, source_target_pairs={{8,0},{16,8},{24,16},{32,24},{40,32},{48,40},{56,48},{64,56},{72,6... | collective-permute-start | bytes 1160 | tf_op jit(solution)/shard_map/ppermute | solution.py:25
  19.4 31.3 %collective-permute-start.6 = (s32[96]{0:T(128)}, s32[96]{0:T(128)}, u32[]{:S(2)}, u32[]{:S(2)}) collective-permute-start(s32[96]{0:T(128)} %get-tuple-element.68), channel_id=1, source_target_pairs={{752,0},{760,8},{0,16},{8,24},{16,32},{24,40},{32,48},{40,56},{48,... | collective-permute-start | bytes 1160 | tf_op jit(solution)/shard_map/ppermute | solution.py:25
  21.4 35.3 %collective-permute-start.4 = (s32[96]{0:T(128)}, s32[96]{0:T(128)}, u32[]{:S(2)}, u32[]{:S(2)}) collective-permute-start(s32[96]{0:T(128)} %get-tuple-element.69), channel_id=1, source_target_pairs={{760,0},{0,8},{8,16},{16,24},{24,32},{32,40},{40,48},{48,56},{56,6... | collective-permute-start | bytes 1160 | tf_op jit(solution)/shard_map/ppermute | solution.py:25
  23.3 19.5 %collective-permute-start = (s32[96]{0:T(128)}, s32[96]{0:T(128)}, u32[]{:S(2)}, u32[]{:S(2)}) collective-permute-start(s32[96]{0:T(128)} %get-tuple-element.70), channel_id=1, source_target_pairs={{16,0},{24,8},{32,16},{40,24},{48,32},{56,40},{64,48},{72,56},{80,... | collective-permute-start | bytes 1160 | tf_op jit(solution)/shard_map/ppermute | solution.py:25
  31.9 1.8 %copy-start.14 = (f32[64,64,1]{0,1,2:T(8,128)S(1)}, f32[64,64,1]{0,1,2:T(8,128)}, u32[]{:S(2)}) copy-start(f32[64,64,1]{0,1,2:T(8,128)} %constant.192) | copy-start | bytes 49156
  31.9 2.1 %copy-start.13 = (f32[64,64,1]{0,1,2:T(8,128)S(1)}, f32[64,64,1]{0,1,2:T(8,128)}, u32[]{:S(2)}) copy-start(f32[64,64,1]{0,1,2:T(8,128)} %constant.193) | copy-start | bytes 49156
  31.9 2.4 %copy-start.12 = (f32[64,64,1]{0,1,2:T(8,128)S(1)}, f32[64,64,1]{0,1,2:T(8,128)}, u32[]{:S(2)}) copy-start(f32[64,64,1]{0,1,2:T(8,128)} %constant.194) | copy-start | bytes 49156
  33.6 1.0 copy-start.11
  33.6 1.3 %copy-start.10 = (f32[64,64,1]{0,1,2:T(8,128)S(1)}, f32[64,64,1]{0,1,2:T(8,128)}, u32[]{:S(2)}) copy-start(f32[64,64,1]{0,1,2:T(8,128)} %constant.196) | copy-start | bytes 49156
  33.6 1.6 %copy-start.9 = (f32[64,64,1]{0,1,2:T(8,128)S(1)}, f32[64,64,1]{0,1,2:T(8,128)}, u32[]{:S(2)}) copy-start(f32[64,64,1]{0,1,2:T(8,128)} %constant.197) | copy-start | bytes 49156
  34.0 1.6 %copy-start.8 = (f32[64,64,1]{0,1,2:T(8,128)S(1)}, f32[64,64,1]{0,1,2:T(8,128)}, u32[]{:S(2)}) copy-start(f32[64,64,1]{0,1,2:T(8,128)} %constant.198) | copy-start | bytes 49156
  34.3 1.6 %copy-start.7 = (f32[64,64,1]{0,1,2:T(8,128)S(1)}, f32[64,64,1]{0,1,2:T(8,128)}, u32[]{:S(2)}) copy-start(f32[64,64,1]{0,1,2:T(8,128)} %constant.199) | copy-start | bytes 49156
  35.3 3.3 %copy-start.16 = (s32[128,1]{0,1:T(1,128)S(1)}, s32[128,1]{0,1:T(1,128)}, u32[]{:S(2)}) copy-start(s32[128,1]{0,1:T(1,128)} %param.25) | copy-start | bytes 1540
  35.3 3.3 %copy-start.6 = (f32[128,3,512]{2,0,1:T(8,128)S(1)}, f32[128,3,512]{2,0,1:T(8,128)}, u32[]{:S(2)}) copy-start(f32[128,3,512]{2,0,1:T(8,128)} %param.20) | copy-start | bytes 2359300
  36.6 9.5 %collective-permute-start.1 = (bf16[96,320]{0,1:T(8,128)(2,1)S(1)}, bf16[96,320]{0,1:T(8,128)(2,1)S(1)}, u32[]{:S(2)}, u32[]{:S(2)}) collective-permute-start(bf16[96,320]{0,1:T(8,128)(2,1)S(1)} %get-tuple-element.66), channel_id=1, source_target_pairs={{16,0},{24,8},{32,16},{40,24},{48,32},{56,40},{64,48},{72,56},{80,... | collective-permute-start | bytes 184328 | tf_op jit(solution)/shard_map/ppermute | solution.py:25
  42.8 17.8 %collective-permute-start.3 = (bf16[96,320]{0,1:T(8,128)(2,1)S(1)}, bf16[96,320]{0,1:T(8,128)(2,1)S(1)}, u32[]{:S(2)}, u32[]{:S(2)}) collective-permute-start(bf16[96,320]{0,1:T(8,128)(2,1)S(1)} %get-tuple-element.63), channel_id=1, source_target_pairs={{8,0},{16,8},{24,16},{32,24},{40,32},{48,40},{56,48},{64,56},{72,6... | collective-permute-start | bytes 184328 | tf_op jit(solution)/shard_map/ppermute | solution.py:25
  46.2 9.7 %collective-permute-start.7 = (bf16[96,320]{0,1:T(8,128)(2,1)S(1)}, bf16[96,320]{0,1:T(8,128)(2,1)S(1)}, u32[]{:S(2)}, u32[]{:S(2)}) collective-permute-start(bf16[96,320]{0,1:T(8,128)(2,1)S(1)} %get-tuple-element.64), channel_id=1, source_target_pairs={{752,0},{760,8},{0,16},{8,24},{16,32},{24,40},{32,48},{40,56},{48,... | collective-permute-start | bytes 184328 | tf_op jit(solution)/shard_map/ppermute | solution.py:25
  50.7 9.1 %collective-permute-start.5 = (bf16[96,320]{0,1:T(8,128)(2,1)S(1)}, bf16[96,320]{0,1:T(8,128)(2,1)S(1)}, u32[]{:S(2)}, u32[]{:S(2)}) collective-permute-start(bf16[96,320]{0,1:T(8,128)(2,1)S(1)} %get-tuple-element.65), channel_id=1, source_target_pairs={{760,0},{0,8},{8,16},{16,24},{24,32},{32,40},{40,48},{48,56},{56,6... | collective-permute-start | bytes 184328 | tf_op jit(solution)/shard_map/ppermute | solution.py:25
  61.6 7.5 %collective-permute-start.9 = (f32[1,5,8,8]{0,3,2,1:T(8,128)S(1)}, f32[1,5,8,8]{0,3,2,1:T(8,128)S(1)}, u32[]{:S(2)}, u32[]{:S(2)}) collective-permute-start(f32[1,5,8,8]{0,3,2,1:T(8,128)S(1)} %get-tuple-element.55), channel_id=1, source_target_pairs={{0,1},{1,2},{2,3},{3,4},{4,5},{5,6},{6,7},{7,8},{8,9},{9,10},{10,1... | collective-permute-start | bytes 3848 | tf_op jit(solution)/shard_map/ppermute | solution.py:33
  66.3 8.4 %collective-permute-start.8 = (f32[1,5,8,8]{0,3,2,1:T(8,128)S(1)}, f32[1,5,8,8]{0,3,2,1:T(8,128)S(1)}, u32[]{:S(2)}, u32[]{:S(2)}) collective-permute-start(f32[1,5,8,8]{0,3,2,1:T(8,128)S(1)} %get-tuple-element.56), channel_id=1, source_target_pairs={{1,0},{2,1},{3,2},{4,3},{5,4},{6,5},{7,6},{8,7},{9,8},{10,9},{11,1... | collective-permute-start | bytes 3848 | tf_op jit(solution)/shard_map/ppermute | solution.py:36
  76.9 0.7 copy-start.15
  83.2 2.9 %copy-start.3 = (f32[128,512]{1,0:T(8,128)S(1)}, f32[128,512]{1,0:T(8,128)}, u32[]{:S(2)}) copy-start(f32[128,512]{1,0:T(8,128)} %copy.62) | copy-start | bytes 786436
  83.2 2.9 %copy-start.5 = (f32[128,512]{1,0:T(8,128)S(1)}, f32[128,512]{1,0:T(8,128)}, u32[]{:S(2)}) copy-start(f32[128,512]{1,0:T(8,128)} %get-tuple-element.62) | copy-start | bytes 786436
  86.1 5.7 %copy-start = (f32[128,5,512]{2,0,1:T(8,128)S(1)}, f32[128,5,512]{2,0,1:T(8,128)}, u32[]{:S(2)}) copy-start(f32[128,5,512]{2,0,1:T(8,128)} %copy.65) | copy-start | bytes 3932164
  86.1 5.7 %copy-start.2 = (f32[512,512,1]{1,0,2:T(8,128)S(1)}, f32[512,512,1]{1,0,2:T(8,128)}, u32[]{:S(2)}) copy-start(f32[512,512,1]{1,0,2:T(8,128)} %constant.201) | copy-start | bytes 3145732
  91.8 2.3 %copy-start.1 = (f32[512,512,1]{1,0,2:T(8,128)S(1)}, f32[512,512,1]{1,0,2:T(8,128)}, u32[]{:S(2)}) copy-start(f32[512,512,1]{1,0,2:T(8,128)} %constant.202) | copy-start | bytes 3145732
  91.8 2.3 %copy-start.4 = (f32[128,512]{1,0:T(8,128)S(1)}, f32[128,512]{1,0:T(8,128)}, u32[]{:S(2)}) copy-start(f32[128,512]{1,0:T(8,128)} %get-tuple-element.60) | copy-start | bytes 786436
where the time goes:
time: 103 us; the launch traced here: 102 us
  starting transfers between devices  44.9 us (44%)
  matrix products  26.4 us (26%)
  local copies, waits for them, and re-layouts  13 us (13%)
  waiting for transfers between devices  12.5 us (12%)
  other arithmetic  4.52 us (4%)
    ppermute x8, starting transfers between devices, passed_along(): return lax.ppermute(block, axis, route)  38.1 us
    dot_general x2, matrix products, derive(): jnp.einsum('efp,qp->efq', field, kron_mat, precision=lax.Precision.HIGHEST)  10.3 us
    ppermute x8, waiting for transfers between devices, passed_along(): return lax.ppermute(block, axis, route)  6.35 us
    ppermute x1, waiting for transfers between devices, extended(): lax.ppermute(lax.slice_in_dim(block, 0, width, axis=dim), axis, backward)  5.61 us
    dot_general x2, matrix products, derive_back(): jnp.einsum('efq,qp->efp', field, kron_mat, precision=lax.Precision.HIGHEST)  5.59 us
    ppermute x1, starting transfers between devices, extended(): lax.ppermute(lax.slice_in_dim(block, block.shape[dim] - width, None, axis...  4.7 us
    dot_general x5, matrix products, absorb(): return total + jnp.dot(hit, faces, preferred_element_type=jnp.float32)  3.54 us
    dot_general x1, matrix products, derive(): jnp.einsum('ai,efip->efap', dmat, cube, precision=lax.Precision.HIGHEST)  3.11 us
  transfers between devices with their start and end apart: 10, of which 4 were waited for; matrix products, arithmetic and copies ran while one was open for 12% of the time, Pallas kernels for 0%

commit v1 on v0

v1 whole, which is shorter than its diff:
```python
import functools

import jax
import jax.numpy as jnp
import ml_dtypes
import numpy as np
from jax import lax
from jax.experimental import pallas as pl
from jax.experimental.pallas import tpu as pltpu
from jax.sharding import PartitionSpec as P

gll_nodes = np.array(
    [
        -1.0,
        -0.8717401485096066,
        -0.5917001814331423,
        -0.2092992179024789,
        0.2092992179024789,
        0.5917001814331423,
        0.8717401485096066,
        1.0,
    ]
)
viscosity = 0.005
OFFSETS = (-2, -1, 1, 2)
BF = jnp.bfloat16
F32 = jnp.float32


def legendre_seven(points):
    prev = np.ones(points.shape)
    curr = np.array(points)
    for order in range(1, 7):
        nxt = ((2 * order + 1) * points * curr - order * prev) / (order + 1)
        prev, curr = (curr, nxt)
    return curr


def diff_matrix():
    values = legendre_seven(gll_nodes)
    mat = np.zeros((8, 8))
    for row in range(8):
        for col in range(8):
            if row != col:
                mat[row, col] = values[row] / (values[col] * (gll_nodes[row] - gll_nodes[col]))
    mat[0, 0] = -14.0
    mat[7, 7] = 14.0
    return mat


def lagrange_at(points):
    basis = np.ones((8, 8))
    for row in range(8):
        for col in range(8):
            for other in range(8):
                if other != col:
                    basis[row, col] *= (points[row] - gll_nodes[other]) / (
                        gll_nodes[col] - gll_nodes[other]
                    )
    return basis


def split(mat):
    mat = np.asarray(mat, np.float32)
    high = mat.astype(ml_dtypes.bfloat16)
    low = (mat - high.astype(np.float32)).astype(ml_dtypes.bfloat16)
    return np.stack([high, low])


def fold_table():
    halves = [lagrange_at((gll_nodes - 1.0) / 2.0), lagrange_at((gll_nodes + 1.0) / 2.0)]
    table = np.zeros((8, 8, 8, 4, 64))
    for code in range(4):
        mat = np.kron(halves[code % 2], halves[code // 2]).astype(np.float32)
        table[:, 7, :, code, :] = mat.reshape(8, 8, 64)
    return split(table.reshape(512, 256))


def turn_table():
    table = np.zeros((2, 64, 2, 2, 64), np.float32)
    for node in range(64):
        table[:, node, 0, :, node] = 1.0
        table[:, (node % 8) * 8 + node // 8, 1, :, node] = 1.0
    return table.reshape(128, 256).astype(ml_dtypes.bfloat16)


def spread_table():
    table = np.zeros((2, 2, 2, 64, 8, 8, 8), np.float32)
    for half in range(2):
        for node in range(64):
            table[half, :, half, node, node // 8, 0, node % 8] = 1.0
    return table.reshape(2, 256, 512).astype(ml_dtypes.bfloat16)


def derivative_tables():
    dmat = diff_matrix().astype(np.float32)
    eye = np.eye(8)
    along_i = np.kron(np.kron(dmat, eye), eye).T
    along_j = np.kron(np.kron(np.eye(4), dmat), eye).T
    along_k = np.kron(np.kron(np.eye(4), eye), dmat).T
    return split(along_i), np.stack([split(along_j), split(along_k)])


def halves_of(value):
    high = value.astype(BF)
    low = (value - high.astype(F32)).astype(BF)
    return high, low


def mm(a, b):
    return jnp.dot(a, b, preferred_element_type=F32)


def mmt(a, b):
    return lax.dot_general(a, b, (((1,), (1,)), ((), ())), preferred_element_type=F32)


ROWS = 336


def exchange_kernel(
    n_dom,
    n_sub,
    x_ref,
    route_ref,
    elem_ref,
    code_ref,
    hang_ref,
    fold_ref,
    turn_ref,
    spread_ref,
    out_ref,
    send,
    got,
    low_send,
    high_send,
    edge_got,
    low_pad,
    high_pad,
    send_sem,
    recv_sem,
    edge_send_sem,
    edge_recv_sem,
):
    dom = lax.axis_index("dom")
    sub = lax.axis_index("sub")
    peers = [{"dom": lax.rem(dom + o + n_dom, n_dom), "sub": sub} for o in OFFSETS]
    place = dom * n_sub + sub
    total = n_dom * n_sub
    before = lax.rem(place + total - 1, total)
    after = lax.rem(place + 1, total)
    prev_dev = {"dom": before // n_sub, "sub": lax.rem(before, n_sub)}
    next_dev = {"dom": after // n_sub, "sub": lax.rem(after, n_sub)}

    barrier = pltpu.get_barrier_semaphore()
    for dev in peers + [prev_dev, next_dev]:
        pl.semaphore_signal(barrier, inc=1, device_id=dev, device_id_type=pl.DeviceIdType.MESH)

    lane = lax.broadcasted_iota(jnp.int32, (128, 128), 1)
    row = lax.broadcasted_iota(jnp.int32, (128, 128), 0)
    left = lane < 64

    def column(ref):
        return jnp.broadcast_to(ref[...].astype(F32), (128, 128)).T

    code = column(code_ref).astype(jnp.int32)
    hang = column(hang_ref)
    quarter = lax.rem(code, 4)
    in_first = quarter < 2
    wanted = jnp.where((lax.rem(quarter, 2) == 0) == left, hang, 0.0)
    turned = code >= 4

    faces = []
    for f in range(5):
        high, low = halves_of(x_ref[f])
        mapped = mm(high, fold_ref[0]) + mm(low, fold_ref[0]) + mm(high, fold_ref[1])
        picked = jnp.where(in_first, mapped[:, :128], mapped[:, 128:]) * wanted
        both = mm(picked.astype(BF), turn_ref[...])
        faces.append(jnp.where(turned, both[:, 128:], both[:, :128]))
    send[0:128, :] = jnp.where(left, faces[0], faces[1]).astype(BF)
    send[128:256, :] = jnp.where(left, faces[2], faces[3]).astype(BF)
    send[256:320, :] = jnp.where(left[:64], faces[4][:64], faces[4][64:]).astype(BF)
    meta_row = lax.broadcasted_iota(jnp.int32, (16, 128), 0)
    send[320:336, :] = jnp.where(
        meta_row == 0,
        jnp.broadcast_to(route_ref[...].astype(F32), (16, 128)),
        jnp.broadcast_to(elem_ref[...].astype(F32), (16, 128)),
    ).astype(BF)

    pl.semaphore_wait(barrier, 6)
    copies = []
    for n, dev in enumerate(peers):
        copy = pltpu.make_async_remote_copy(
            src_ref=send,
            dst_ref=got.at[n],
            send_sem=send_sem.at[n],
            recv_sem=recv_sem.at[n],
            device_id=dev,
            device_id_type=pl.DeviceIdType.MESH,
        )
        copy.start()
        copies.append(copy)

    def absorb(total, block):
        route = block[320:321, :].astype(F32)
        elem = block[321:322, :].astype(F32)
        dest = jnp.where(route == dom.astype(F32), elem, -1.0)
        hit = (jnp.broadcast_to(dest, (128, 128)) == row.astype(F32)).astype(F32).astype(BF)
        tail = block[256:320, :].astype(F32)
        last = jnp.concatenate(
            [jnp.where(left[:64], tail, 0.0), jnp.where(left[:64], 0.0, tail)], axis=0
        ).astype(BF)
        return [
            total[0] + mm(hit, block[0:128, :]),
            total[1] + mm(hit, block[128:256, :]),
            total[2] + mm(hit, last),
        ]

    sums = absorb([jnp.zeros((128, 128), F32)] * 3, send)
    for n, copy in enumerate(copies):
        copy.wait_recv()
        sums = absorb(sums, got.at[n])

    wide_lane = lax.broadcasted_iota(jnp.int32, (128, 512), 1)
    loses = lax.rem(wide_lane, 64) >= 56
    keep = 1.0 - hang
    keep = jnp.where(loses, jnp.concatenate([keep] * 4, axis=1), 1.0)
    packed = []
    for part in sums:
        high, low = halves_of(part)
        packed.append(jnp.concatenate([high, low], axis=1))
    for f in range(5):
        spread = mm(packed[f // 2], spread_ref[f % 2])
        if f == 4:
            spread = spread + mm(packed[2], spread_ref[1])
        value = x_ref[f] * keep + spread
        out_ref[f, :, 128:384] = value[:, 128:384]
        low_pad[f, 8:136, :] = value[:, 0:128]
        high_pad[f, 8:136, :] = value[:, 384:512]
        low_send[f : f + 1, :] = value[0:1, 0:128]
        high_send[f : f + 1, :] = value[127:128, 384:512]

    to_prev = pltpu.make_async_remote_copy(
        src_ref=low_send,
        dst_ref=edge_got.at[0],
        send_sem=edge_send_sem.at[0],
        recv_sem=edge_recv_sem.at[0],
        device_id=prev_dev,
        device_id_type=pl.DeviceIdType.MESH,
    )
    to_prev.start()
    to_next = pltpu.make_async_remote_copy(
        src_ref=high_send,
        dst_ref=edge_got.at[1],
        send_sem=edge_send_sem.at[1],
        recv_sem=edge_recv_sem.at[1],
        device_id=next_dev,
        device_id_type=pl.DeviceIdType.MESH,
    )
    to_next.start()
    to_prev.wait_recv()
    to_next.wait_recv()
    has_next = jnp.where(place < total - 1, 1.0, 0.0)
    has_prev = jnp.where(place > 0, 1.0, 0.0)
    for f in range(5):
        low_pad[f, 136:137, :] = edge_got[0, f : f + 1, :] * has_next
        high_pad[f, 7:8, :] = edge_got[1, f : f + 1, :] * has_prev
        above = low_pad[f, 9:137, :]
        below = high_pad[f, 7:135, :]
        out_ref[f, :, 0:128] = low_pad[f, 8:136, :] + jnp.where(
            left, pltpu.roll(below, 64, 1), 0.0
        )
        out_ref[f, :, 384:512] = high_pad[f, 8:136, :] + jnp.where(
            left, 0.0, pltpu.roll(above, 64, 1)
        )
    for copy in copies:
        copy.wait_send()
    to_prev.wait_send()
    to_next.wait_send()


def operator_kernel(u_ref, metric_ref, velocity_ref, i_ref, jk_ref, out_ref):
    u = u_ref[...].reshape(640, 512)
    high, low = halves_of(u)
    pieces = [slice(0, 256), slice(256, 512)]

    def inner(dim, cols, derived):
        m = metric_ref[dim, :, cols] * viscosity
        v = velocity_ref[dim, :, cols]
        cube = derived.reshape(5, 128, 256)
        value = cube * m[None] + u_ref[:, :, cols] * v[None]
        return halves_of(value.reshape(640, 256))

    parts_i = []
    for cols in pieces:
        derived = jnp.zeros((640, 256), F32)
        for rows in pieces:
            derived += mm(high[:, rows], i_ref[0, rows, cols])
            derived += mm(low[:, rows], i_ref[0, rows, cols])
            derived += mm(high[:, rows], i_ref[1, rows, cols])
        parts_i.append(inner(0, cols, derived))
    for n, cols in enumerate(pieces):
        total = jnp.zeros((640, 256), F32)
        for m, rows in enumerate(pieces):
            a, b = parts_i[m]
            total += mmt(a, i_ref[0, cols, rows])
            total += mmt(b, i_ref[0, cols, rows])
            total += mmt(a, i_ref[1, cols, rows])
        for dim in (1, 2):
            derived = mm(high[:, cols], jk_ref[dim - 1, 0])
            derived += mm(low[:, cols], jk_ref[dim - 1, 0])
            derived += mm(high[:, cols], jk_ref[dim - 1, 1])
            a, b = inner(dim, cols, derived)
            total += mmt(a, jk_ref[dim - 1, 0])
            total += mmt(b, jk_ref[dim - 1, 0])
            total += mmt(a, jk_ref[dim - 1, 1])
        out_ref[:, :, cols] = total.reshape(5, 128, 256)


def shards(n_dom, n_sub, adjoint_field, metric, velocity, route, element, code, hanging):
    x = jnp.transpose(adjoint_field, (1, 0, 2))
    met = jnp.transpose(metric, (1, 0, 2))
    vel = jnp.transpose(velocity, (1, 0, 2))
    rows = [a.reshape(1, 128) for a in (route, element, code, hanging)]
    along_i, along_jk = derivative_tables()
    vmem = pl.BlockSpec(memory_space=pltpu.VMEM)
    u = pl.pallas_call(
        functools.partial(exchange_kernel, n_dom, n_sub),
        out_shape=jax.ShapeDtypeStruct((5, 128, 512), F32),
        in_specs=[vmem] * 8,
        out_specs=vmem,
        scratch_shapes=[
            pltpu.VMEM((ROWS, 128), BF),
            pltpu.VMEM((4, ROWS, 128), BF),
            pltpu.VMEM((8, 128), F32),
            pltpu.VMEM((8, 128), F32),
            pltpu.VMEM((2, 8, 128), F32),
            pltpu.VMEM((5, 144, 128), F32),
            pltpu.VMEM((5, 144, 128), F32),
            pltpu.SemaphoreType.DMA((4,)),
            pltpu.SemaphoreType.DMA((4,)),
            pltpu.SemaphoreType.DMA((2,)),
            pltpu.SemaphoreType.DMA((2,)),
        ],
        compiler_params=pltpu.CompilerParams(
            collective_id=0, has_side_effects=True, vmem_limit_bytes=24 << 20
        ),
        name="exchange",
    )(x, *rows, jnp.asarray(fold_table()), jnp.asarray(turn_table()), jnp.asarray(spread_table()))
    result = pl.pallas_call(
        operator_kernel,
        out_shape=jax.ShapeDtypeStruct((5, 128, 512), F32),
        in_specs=[vmem] * 5,
        out_specs=vmem,
        compiler_params=pltpu.CompilerParams(vmem_limit_bytes=40 << 20),
        name="operator",
    )(u, met, vel, jnp.asarray(along_i), jnp.asarray(along_jk))
    return jnp.transpose(result, (1, 0, 2))


def solution(mesh):
    sizes = dict(zip(mesh.axis_names, mesh.devices.shape))
    block = P(("dom", "sub"), None, None)
    flat = P(("dom", "sub"), None)
    return jax.shard_map(
        functools.partial(shards, sizes["dom"], sizes["sub"]),
        mesh=mesh,
        in_specs=(block, block, block, flat, flat, flat, flat),
        out_specs=block,
        check_vma=False,
    )
```

time: 103 us -> 40.7 us (0.40)
  the two profiles are of different devices: /device:TPU:24 before, /device:TPU:1 now
where the time goes in v1:
time: 40.7 us; the launch traced here: 40.4 us
  Pallas kernels  33.4 us (82%)
  local copies, waits for them, and re-layouts  6.87 us (17%)
    pallas_call x1, Pallas kernels, shards(): pl.pallas_call(functools.partial(exchange_kernel, n_dom, n_sub), out_shap...  27.6 us
    unnamed x24, local copies, waits for them, and re-layouts  6.87 us
    pallas_call x1, Pallas kernels, shards(): pl.pallas_call(operator_kernel, out_shape=jax.ShapeDtypeStruct((5, 128, 5...  5.83 us

profile of v1, /device:TPU:1, one launch (start us, length us, event | category | flops | bytes accessed | tf_op | source)
XLA Modules:
  0.0 40.4 jit_solution(17127321948844842637)
XLA Ops:
  0.0 0.0 copy-start
  0.0 1.3 %copy-done = f32[128,5,512]{2,0,1:T(8,128)S(1)} copy-done((f32[128,5,512]{2,0,1:T(8,128)S(1)}, f32[128,5,512]{2,0,1:T(8,128)}, u32[]{:S(2)}) %copy-start) | copy-done | bytes 1310744
  1.3 0.0 copy-start.4
  1.3 1.0 %copy-done.4 = bf16[2,256,512]{2,1,0:T(8,128)(2,1)S(1)} copy-done((bf16[2,256,512]{2,1,0:T(8,128)(2,1)S(1)}, bf16[2,256,512]{2,1,0:T(8,128)(2,1)}, u32[]{:S(2)}) %copy-start.4) | copy-done | bytes 524312
  2.4 0.0 copy-start.5
  2.4 1.0 %copy-done.5 = bf16[2,512,256]{2,1,0:T(8,128)(2,1)S(1)} copy-done((bf16[2,512,256]{2,1,0:T(8,128)(2,1)S(1)}, bf16[2,512,256]{2,1,0:T(8,128)(2,1)}, u32[]{:S(2)}) %copy-start.5) | copy-done | bytes 524312
  3.4 0.0 copy-start.7
  3.4 0.8 %copy-done.7 = bf16[128,256]{1,0:T(8,128)(2,1)S(1)} copy-done((bf16[128,256]{1,0:T(8,128)(2,1)S(1)}, bf16[128,256]{1,0:T(8,128)(2,1)}, u32[]{:S(2)}) %copy-start.7) | copy-done | bytes 65560
  4.2 0.0 copy-start.8
  4.2 0.7 %copy-done.8 = s32[128,1]{0,1:T(1,128)S(1)} copy-done((s32[128,1]{0,1:T(1,128)S(1)}, s32[128,1]{0,1:T(1,128)}, u32[]{:S(2)}) %copy-start.8) | copy-done | bytes 536
  4.9 0.0 copy-start.9
  4.9 0.7 %copy-done.9 = s32[128,1]{0,1:T(1,128)S(1)} copy-done((s32[128,1]{0,1:T(1,128)S(1)}, s32[128,1]{0,1:T(1,128)}, u32[]{:S(2)}) %copy-start.9) | copy-done | bytes 536
  5.6 0.0 copy-start.10
  5.6 0.7 %copy-done.10 = s32[128,1]{0,1:T(1,128)S(1)} copy-done((s32[128,1]{0,1:T(1,128)S(1)}, s32[128,1]{0,1:T(1,128)}, u32[]{:S(2)}) %copy-start.10) | copy-done | bytes 536
  6.2 0.0 copy-start.11
  6.2 0.7 %copy-done.11 = s32[128,1]{0,1:T(1,128)S(1)} copy-done((s32[128,1]{0,1:T(1,128)S(1)}, s32[128,1]{0,1:T(1,128)}, u32[]{:S(2)}) %copy-start.11) | copy-done | bytes 536
  6.9 0.0 copy-start.1
  6.9 0.0 copy-start.2
  6.9 0.0 copy-start.3
  6.9 0.0 copy-start.6
  6.9 27.6 %exchange.1.u_ref = f32[5,128,512]{2,1,0:T(8,128)S(1)} custom-call(f32[5,128,512]{2,1,0:T(8,128)S(1)} %bitcast.8, s32[1,128]{1,0:T(1,128)S(1)} %bitcast.11, s32[1,128]{1,0:T(1,128)S(1)} %bitcast.12, s32[1,128]{1,0:T(1,128)S(1)} %bitcast.13, s32[1,128]{1,0:T(1,128)S(1)} %bitcast.14, bf16[2,512,256]{2,1,0:T(8,128)(2,1)S(1)} %copy-done.5, ...), custom_call_target="tpu_custom_call" | custom-call | tf_op jit(solution)/shard_map/exchange/pallas_call | solution.py:327
  34.5 0.0 copy-done.1
  34.5 0.0 copy-done.2
  34.5 0.0 copy-done.3
  34.5 0.0 copy-done.6
  34.5 5.8 %operator.1 = f32[5,128,512]{2,1,0:T(8,128)} custom-call(f32[5,128,512]{2,1,0:T(8,128)S(1)} %exchange.1.u_ref, f32[3,128,512]{2,1,0:T(8,128)S(1)} %bitcast.9, f32[3,128,512]{2,1,0:T(8,128)S(1)} %bitcast.10, bf16[2,512,512]{2,1,0:T(8,128)(2,1)S(1)} %copy-done.1, bf16[2,2,256,256]{3,2,1,0:T(8,128)(2,1)S(1)} %copy-done.6), custom_call_target="tpu_custom_call" | custom-call | tf_op jit(solution)/shard_map/operator/pallas_call | solution.py:350
Async XLA Ops:
  0.0 1.3 %copy-start = (f32[128,5,512]{2,0,1:T(8,128)S(1)}, f32[128,5,512]{2,0,1:T(8,128)}, u32[]{:S(2)}) copy-start(f32[128,5,512]{2,0,1:T(8,128)} %param.12) | copy-start | bytes 3932164
  1.3 1.0 %copy-start.4 = (bf16[2,256,512]{2,1,0:T(8,128)(2,1)S(1)}, bf16[2,256,512]{2,1,0:T(8,128)(2,1)}, u32[]{:S(2)}) copy-start(bf16[2,256,512]{2,1,0:T(8,128)(2,1)} %constant.12.clone.spread_ref) | copy-start | bytes 1572868
  2.4 1.0 %copy-start.5 = (bf16[2,512,256]{2,1,0:T(8,128)(2,1)S(1)}, bf16[2,512,256]{2,1,0:T(8,128)(2,1)}, u32[]{:S(2)}) copy-start(bf16[2,512,256]{2,1,0:T(8,128)(2,1)} %constant.10.clone.fold_ref) | copy-start | bytes 1572868
  3.4 0.8 %copy-start.7 = (bf16[128,256]{1,0:T(8,128)(2,1)S(1)}, bf16[128,256]{1,0:T(8,128)(2,1)}, u32[]{:S(2)}) copy-start(bf16[128,256]{1,0:T(8,128)(2,1)} %constant.11.clone.turn_ref) | copy-start | bytes 196612
  4.2 0.7 %copy-start.8 = (s32[128,1]{0,1:T(1,128)S(1)}, s32[128,1]{0,1:T(1,128)}, u32[]{:S(2)}) copy-start(s32[128,1]{0,1:T(1,128)} %param.15) | copy-start | bytes 1540
  4.9 0.7 %copy-start.9 = (s32[128,1]{0,1:T(1,128)S(1)}, s32[128,1]{0,1:T(1,128)}, u32[]{:S(2)}) copy-start(s32[128,1]{0,1:T(1,128)} %param.16) | copy-start | bytes 1540
  5.6 0.7 %copy-start.10 = (s32[128,1]{0,1:T(1,128)S(1)}, s32[128,1]{0,1:T(1,128)}, u32[]{:S(2)}) copy-start(s32[128,1]{0,1:T(1,128)} %param.17) | copy-start | bytes 1540
  6.2 0.7 %copy-start.11 = (s32[128,1]{0,1:T(1,128)S(1)}, s32[128,1]{0,1:T(1,128)}, u32[]{:S(2)}) copy-start(s32[128,1]{0,1:T(1,128)} %param.18) | copy-start | bytes 1540
  6.9 27.6 %copy-start.1 = (bf16[2,512,512]{2,1,0:T(8,128)(2,1)S(1)}, bf16[2,512,512]{2,1,0:T(8,128)(2,1)}, u32[]{:S(2)}) copy-start(bf16[2,512,512]{2,1,0:T(8,128)(2,1)} %constant.13.clone.i_ref) | copy-start | bytes 3145732
  6.9 27.6 %copy-start.2 = (f32[128,3,512]{2,0,1:T(8,128)S(1)}, f32[128,3,512]{2,0,1:T(8,128)}, u32[]{:S(2)}) copy-start(f32[128,3,512]{2,0,1:T(8,128)} %param.13) | copy-start | bytes 2359300
  6.9 27.6 %copy-start.3 = (f32[128,3,512]{2,0,1:T(8,128)S(1)}, f32[128,3,512]{2,0,1:T(8,128)}, u32[]{:S(2)}) copy-start(f32[128,3,512]{2,0,1:T(8,128)} %param.14) | copy-start | bytes 2359300
  6.9 27.6 %copy-start.6 = (bf16[2,2,256,256]{3,2,1,0:T(8,128)(2,1)S(1)}, bf16[2,2,256,256]{3,2,1,0:T(8,128)(2,1)}, u32[]{:S(2)}) copy-start(bf16[2,2,256,256]{3,2,1,0:T(8,128)(2,1)} %constant.14.clone.jk_ref) | copy-start | bytes 1572868

commit v2 on v1

v2 whole, which is shorter than its diff:
```python
import functools

import jax
import jax.numpy as jnp
import ml_dtypes
import numpy as np
from jax import lax
from jax.experimental import pallas as pl
from jax.experimental.pallas import tpu as pltpu
from jax.sharding import PartitionSpec as P

gll_nodes = np.array(
    [
        -1.0,
        -0.8717401485096066,
        -0.5917001814331423,
        -0.2092992179024789,
        0.2092992179024789,
        0.5917001814331423,
        0.8717401485096066,
        1.0,
    ]
)
viscosity = 0.005
OFFSETS = (-2, -1, 1, 2)
BF = jnp.bfloat16
F32 = jnp.float32


def legendre_seven(points):
    prev = np.ones(points.shape)
    curr = np.array(points)
    for order in range(1, 7):
        nxt = ((2 * order + 1) * points * curr - order * prev) / (order + 1)
        prev, curr = (curr, nxt)
    return curr


def diff_matrix():
    values = legendre_seven(gll_nodes)
    mat = np.zeros((8, 8))
    for row in range(8):
        for col in range(8):
            if row != col:
                mat[row, col] = values[row] / (values[col] * (gll_nodes[row] - gll_nodes[col]))
    mat[0, 0] = -14.0
    mat[7, 7] = 14.0
    return mat


def lagrange_at(points):
    basis = np.ones((8, 8))
    for row in range(8):
        for col in range(8):
            for other in range(8):
                if other != col:
                    basis[row, col] *= (points[row] - gll_nodes[other]) / (
                        gll_nodes[col] - gll_nodes[other]
                    )
    return basis


def split(mat):
    mat = np.asarray(mat, np.float32)
    high = mat.astype(ml_dtypes.bfloat16)
    low = (mat - high.astype(np.float32)).astype(ml_dtypes.bfloat16)
    return np.stack([high, low])


def fold_table():
    parts = [lagrange_at((gll_nodes - 1.0) / 2.0), lagrange_at((gll_nodes + 1.0) / 2.0)]
    turn = np.zeros((64, 64))
    for col in range(64):
        turn[col % 8 * 8 + col // 8, col] = 1.0
    mats = []
    for code in range(8):
        mat = np.kron(parts[code % 2], parts[code // 2 % 2])
        mats.append(mat @ turn if code >= 4 else mat)
    high, low = split(np.stack(mats, axis=1))
    table = np.zeros((2, 2, 8, 8, 8, 64), np.float32)
    for i in range(8):
        a, b = divmod(i, 2)
        rows = slice(8 * i, 8 * i + 8)
        table[0, b, 7 - a] = high[rows].astype(np.float32)
        table[0, b, 3 - a] = high[rows].astype(np.float32)
        table[1, b, 7 - a] = low[rows].astype(np.float32)
    return table.reshape(256, 512).astype(ml_dtypes.bfloat16)


def face_derivatives(dmat):
    eye = np.eye(8)
    return np.kron(dmat, eye).T, np.kron(eye, dmat).T


def to_low_face():
    table = np.zeros((8, 8, 8, 8, 8))
    for i in range(8):
        for k in range(8):
            table[i, k, i, 0, k] = 1.0
    return table.reshape(64, 512)


def tables():
    dmat = diff_matrix().astype(np.float32)
    eye = np.eye(8)
    along_i = np.kron(np.kron(dmat, eye), eye).T
    along_j = np.kron(np.kron(np.eye(4), dmat), eye).T
    along_k = np.kron(np.kron(np.eye(4), eye), dmat).T
    i_tab = split(along_i)
    jk_tab = np.stack([split(along_j), split(along_k)])

    first, second = face_derivatives(dmat)
    both = np.concatenate([first, second], axis=1)
    zero = np.zeros((64, 128))
    high, low = [t.astype(np.float32) for t in split(both)]
    pair_high = np.block([[high, zero], [zero, high]])
    pair_low = np.block([[low, zero], [zero, low]])
    forward = np.stack(
        [np.concatenate([pair_high, pair_high]), np.concatenate([pair_low, 0 * pair_low])]
    )
    single = np.concatenate([high, low, high, 0 * high])
    back = both.T
    spread = to_low_face()
    bh, bl = [t.astype(np.float32) for t in split(back)]
    down = np.stack(
        [np.concatenate([bh, bh]) @ spread, np.concatenate([bl, 0 * bl]) @ spread]
    )
    twice = np.concatenate([np.eye(64), np.eye(64)], axis=1)
    single_back = np.stack(
        [np.concatenate([bh, bh]) @ twice, np.concatenate([bl, 0 * bl]) @ twice]
    )
    every = np.zeros((8, 8, 8, 8, 8))
    for i in range(8):
        for k in range(8):
            every[i, k, i, :, k] = 1.0
    every = every.reshape(64, 512)
    none = np.zeros((64, 512))
    expand = np.stack(
        [
            np.concatenate([every, none, every, none]),
            np.concatenate([none, every, none, every]),
        ]
    )
    gather = spread.T
    blank = np.zeros((512, 64))
    pick = np.concatenate([gather, blank, blank, gather], axis=1)
    cast = lambda t: np.asarray(t, np.float32).astype(ml_dtypes.bfloat16)
    vecs = np.zeros((8, 8, 8, 8), np.float32)
    vecs[0] = dmat[:, 0][None, :, None]
    vecs[1] = dmat[:, 0][:, None, None]
    vecs[2] = dmat[:, 7][:, None, None]
    late = np.concatenate(
        [expand[0], expand[1], down[0], down[1], forward[0], forward[1], single]
        + [single_back[0], single_back[1], np.zeros((256, 128))],
        axis=1,
    )
    return (
        fold_table(),
        i_tab,
        jk_tab,
        cast(pick),
        cast(late),
        vecs.reshape(8, 512),
    )


def halves_of(value):
    high = value.astype(BF)
    low = (value - high.astype(F32)).astype(BF)
    return high, low


def mm(a, b):
    return jnp.dot(a, b, preferred_element_type=F32)


def mmt(a, b):
    return lax.dot_general(a, b, (((1,), (1,)), ((), ())), preferred_element_type=F32)


def side_by_side(value):
    return jnp.concatenate(halves_of(value), axis=1)


ROWS = 336
HALF = [slice(0, 256), slice(256, 512)]
EXPAND, DOWN, FORWARD, SINGLE, SINGLE_BACK = 0, 1024, 2048, 2560, 2688


def apply_operator(x, met, vel, i_tab, jk_tab, out_ref):
    high, low = halves_of(x[...].reshape(640, 512))

    def inner(dim, cols, derived):
        m = met[dim, :, cols] * viscosity
        v = vel[dim, :, cols]
        value = derived.reshape(5, 128, 256) * m[None] + x[:, :, cols] * v[None]
        return halves_of(value.reshape(640, 256))

    parts_i = []
    for cols in HALF:
        derived = jnp.zeros((640, 256), F32)
        for rows in HALF:
            derived += mm(high[:, rows], i_tab[0, rows, cols])
            derived += mm(low[:, rows], i_tab[0, rows, cols])
            derived += mm(high[:, rows], i_tab[1, rows, cols])
        parts_i.append(inner(0, cols, derived))
    for cols in HALF:
        total = jnp.zeros((640, 256), F32)
        for m, rows in enumerate(HALF):
            a, b = parts_i[m]
            total += mmt(a, i_tab[0, cols, rows])
            total += mmt(b, i_tab[0, cols, rows])
            total += mmt(a, i_tab[1, cols, rows])
        for dim in (1, 2):
            derived = mm(high[:, cols], jk_tab[dim - 1, 0])
            derived += mm(low[:, cols], jk_tab[dim - 1, 0])
            derived += mm(high[:, cols], jk_tab[dim - 1, 1])
            a, b = inner(dim, cols, derived)
            total += mmt(a, jk_tab[dim - 1, 0])
            total += mmt(b, jk_tab[dim - 1, 0])
            total += mmt(a, jk_tab[dim - 1, 1])
        out_ref[:, :, cols] = total.reshape(5, 128, 256)


def kernel(n_dom, n_sub, *refs):
    (x_hbm, met_hbm, vel_hbm, route_hbm, elem_hbm, code_hbm, hang_hbm) = refs[:7]
    (fold_hbm, i_hbm, jk_hbm, pick_hbm, late_hbm, vecs_hbm) = refs[7:13]
    out_ref = refs[13]
    (x, met, vel, route_ref, elem_ref, code_ref, hang_ref) = refs[14:21]
    (fold, i_tab, jk_tab, pick, late, vecs) = refs[21:27]
    (send, got, low_send, high_send, edge_got, low_pad, high_pad, mortar_pad) = refs[27:35]
    (w_ref, face_met, face_vel, wi_ref, edge_met, edge_vel) = refs[35:41]
    (load_sem, send_sem, recv_sem, edge_send_sem, edge_recv_sem) = refs[41:46]

    dom = lax.axis_index("dom")
    sub = lax.axis_index("sub")
    mesh_id = pl.DeviceIdType.MESH
    peers = [{"dom": lax.rem(dom + o + n_dom, n_dom), "sub": sub} for o in OFFSETS]
    place = dom * n_sub + sub
    total = n_dom * n_sub
    before = lax.rem(place + total - 1, total)
    after = lax.rem(place + 1, total)
    prev_dev = {"dom": before // n_sub, "sub": lax.rem(before, n_sub)}
    next_dev = {"dom": after // n_sub, "sub": lax.rem(after, n_sub)}

    loads = []

    def load(src, dst):
        copy = pltpu.make_async_copy(src, dst, load_sem.at[len(loads)])
        copy.start()
        loads.append(copy)
        return copy

    x_loads = [load(x_hbm, x)]
    first_loads = [
        load(fold_hbm, fold),
        load(code_hbm, code_ref),
        load(hang_hbm, hang_ref),
        load(route_hbm, route_ref),
        load(elem_hbm, elem_ref),
    ]
    barrier = pltpu.get_barrier_semaphore()
    for dev in peers + [prev_dev, next_dev]:
        pl.semaphore_signal(barrier, inc=1, device_id=dev, device_id_type=mesh_id)
    later_loads = [
        load(i_hbm, i_tab),
        load(jk_hbm, jk_tab),
        load(met_hbm, met),
        load(vel_hbm, vel),
        load(pick_hbm, pick),
        load(late_hbm, late),
        load(vecs_hbm, vecs),
    ]

    lane = lax.broadcasted_iota(jnp.int32, (128, 128), 1)
    row = lax.broadcasted_iota(jnp.int32, (128, 128), 0)
    left = lane < 64
    slot = lax.rem(lane, 64) // 8

    low_send[...] = jnp.zeros((8, 128), F32)
    high_send[...] = jnp.zeros((8, 128), F32)
    for f in range(5):
        low_pad[f, 136:144, :] = jnp.zeros((8, 128), F32)
        high_pad[f, 0:8, :] = jnp.zeros((8, 128), F32)
    for c in range(3):
        mortar_pad[c, 0:8, :] = jnp.zeros((8, 128), F32)
        mortar_pad[c, 136:144, :] = jnp.zeros((8, 128), F32)

    for copy in first_loads:
        copy.wait()

    def column(ref):
        return jnp.broadcast_to(ref[...].astype(F32), (128, 128)).T

    code = column(code_ref).astype(jnp.int32)
    hang = column(hang_ref)
    odd = lax.rem(code, 2) == 1

    for copy in x_loads:
        copy.wait()
    faces = []
    for f in range(5):
        packed = jnp.where(
            slot == 7,
            x[f, :, 0:128],
            jnp.where(
                slot == 6,
                pltpu.roll(x[f, :, 128:256], 120, 1),
                jnp.where(
                    slot == 5,
                    pltpu.roll(x[f, :, 256:384], 112, 1),
                    pltpu.roll(x[f, :, 384:512], 104, 1),
                ),
            ),
        )
        high = packed.astype(BF)
        low = packed - high.astype(F32)
        mixed = jnp.where(slot >= 4, packed, pltpu.roll(low, 96, 1)).astype(BF)
        mapped = mm(jnp.concatenate([mixed, high], axis=1), fold[...])
        picked = jnp.where(
            code < 4,
            jnp.where(code < 2, mapped[:, 0:128], mapped[:, 128:256]),
            jnp.where(code < 6, mapped[:, 256:384], mapped[:, 384:512]),
        )
        picked = picked * hang
        other = pltpu.roll(picked, 64, 1)
        faces.append((jnp.where(odd, other, picked), jnp.where(odd, picked, other)))
    send[0:128, :] = jnp.where(left, faces[0][0], faces[1][1]).astype(BF)
    send[128:256, :] = jnp.where(left, faces[2][0], faces[3][1]).astype(BF)
    send[256:320, :] = jnp.where(left[:64], faces[4][0][:64], faces[4][1][64:]).astype(BF)
    meta_row = lax.broadcasted_iota(jnp.int32, (16, 128), 0)
    send[320:336, :] = jnp.where(
        meta_row == 0,
        jnp.broadcast_to(route_ref[...].astype(F32), (16, 128)),
        jnp.broadcast_to(elem_ref[...].astype(F32), (16, 128)),
    ).astype(BF)

    pl.semaphore_wait(barrier, 6)
    copies = []
    for n, dev in enumerate(peers):
        copy = pltpu.make_async_remote_copy(
            src_ref=send,
            dst_ref=got.at[n],
            send_sem=send_sem.at[n],
            recv_sem=recv_sem.at[n],
            device_id=dev,
            device_id_type=mesh_id,
        )
        copy.start()
        copies.append(copy)

    keep = 1.0 - hang
    keep = jnp.where(slot == 7, keep, 1.0)
    for f in range(5):
        x[f, :, 128:256] = x[f, :, 128:256] * keep
        x[f, :, 256:384] = x[f, :, 256:384] * keep
        low_pad[f, 8:136, :] = x[f, :, 0:128] * keep
        high_pad[f, 8:136, :] = x[f, :, 384:512] * keep
        above = low_pad[f, 9:137, :]
        below = high_pad[f, 7:135, :]
        x[f, :, 0:128] = low_pad[f, 8:136, :] + jnp.where(left, pltpu.roll(below, 64, 1), 0.0)
        x[f, :, 384:512] = high_pad[f, 8:136, :] + jnp.where(left, 0.0, pltpu.roll(above, 64, 1))
    for copy in later_loads:
        copy.wait()
    apply_operator(x, met, vel, i_tab, jk_tab, out_ref)

    wide = lax.broadcasted_iota(jnp.int32, (128, 512), 1)
    on_low = lax.rem(wide, 64) < 8
    weight = met[1] * viscosity * vecs[0:1, :] + jnp.where(on_low, vel[1], 0.0)
    wh, wl = halves_of(weight)
    for cols in HALF:
        w_ref[:, cols] = (
            mmt(wh[:, cols], jk_tab[0, 0])
            + mmt(wl[:, cols], jk_tab[0, 0])
            + mmt(wh[:, cols], jk_tab[0, 1])
        )

    def low_nodes(src):
        ah, al = halves_of(src[0])
        bh, bl = halves_of(src[2])
        return (
            mm(ah, pick[:, 0:128])
            + mm(al, pick[:, 0:128])
            + mm(bh, pick[:, 128:256])
            + mm(bl, pick[:, 128:256])
        )

    face_met[...] = low_nodes(met) * viscosity
    face_vel[...] = low_nodes(vel)

    edge_rows = lax.broadcasted_iota(jnp.int32, (16, 512), 0)
    edge_wide = lax.broadcasted_iota(jnp.int32, (16, 512), 1)
    head = edge_rows < 8

    def ends(src, dim):
        a = jnp.broadcast_to(src[dim, 0:1, :], (16, 512))
        b = jnp.broadcast_to(src[dim, 127:128, :], (16, 512))
        return a, b

    ma, mb = ends(met, 0)
    va, vb = ends(vel, 0)
    ea = ma * viscosity * vecs[1:2, :] + jnp.where(edge_wide < 64, va, 0.0)
    eb = mb * viscosity * vecs[2:3, :] + jnp.where(edge_wide >= 448, vb, 0.0)
    eh, el = halves_of(jnp.where(head, ea, eb))
    for cols in HALF:
        acc = jnp.zeros((16, 256), F32)
        for rows in HALF:
            acc += mmt(eh[:, rows], i_tab[0, cols, rows])
            acc += mmt(el[:, rows], i_tab[0, cols, rows])
            acc += mmt(eh[:, rows], i_tab[1, cols, rows])
        wi_ref[:, cols] = acc
    left16 = left[:16]
    head16 = row[:16] < 8

    def end_faces(src):
        j0, j7 = ends(src, 1)
        k0, k7 = ends(src, 2)
        a = jnp.where(left16, j0[:, 0:128], pltpu.roll(k0[:, 0:128], 64, 1))
        b = jnp.where(left16, pltpu.roll(j7[:, 384:512], 64, 1), k7[:, 384:512])
        return jnp.where(head16, a, b)

    edge_met[...] = end_faces(met) * viscosity
    edge_vel[...] = end_faces(vel)

    def absorb(sums, block):
        route = block[320:321, :].astype(F32)
        elem = block[321:322, :].astype(F32)
        dest = jnp.where(route == dom.astype(F32), elem, -1.0)
        hit = (jnp.broadcast_to(dest, (128, 128)) == row.astype(F32)).astype(F32).astype(BF)
        tail = block[256:320, :].astype(F32)
        last = jnp.concatenate(
            [jnp.where(left[:64], tail, 0.0), jnp.where(left[:64], 0.0, tail)], axis=0
        ).astype(BF)
        return [
            sums[0] + mm(hit, block[0:128, :]),
            sums[1] + mm(hit, block[128:256, :]),
            sums[2] + mm(hit, last),
        ]

    sums = absorb([jnp.zeros((128, 128), F32)] * 3, send)
    for n, copy in enumerate(copies):
        copy.wait_recv()
        sums = absorb(sums, got.at[n])
    sums[2] = sums[2] + pltpu.roll(sums[2], 64, 1)

    lane8 = lane[:8]
    for f in range(5):
        part = sums[f // 2]
        top, bottom = part[0:8, :], part[120:128, :]
        shift_low, shift_high = (64, 72) if f % 2 else (0, 8)
        if shift_low:
            top = pltpu.roll(top, shift_low, 1)
        bottom = pltpu.roll(bottom, shift_high, 1)
        top = jnp.where(lane8 < 8, top, 0.0)
        bottom = jnp.where((lane8 >= 64) & (lane8 < 72), bottom, 0.0)
        low_send[f : f + 1, :] = low_pad[f, 8:9, :] + top[0:1, :]
        high_send[f : f + 1, :] = high_pad[f, 135:136, :] + bottom[7:8, :]
    to_prev = pltpu.make_async_remote_copy(
        src_ref=low_send,
        dst_ref=edge_got.at[0],
        send_sem=edge_send_sem.at[0],
        recv_sem=edge_recv_sem.at[0],
        device_id=prev_dev,
        device_id_type=mesh_id,
    )
    to_prev.start()
    to_next = pltpu.make_async_remote_copy(
        src_ref=high_send,
        dst_ref=edge_got.at[1],
        send_sem=edge_send_sem.at[1],
        recv_sem=edge_recv_sem.at[1],
        device_id=next_dev,
        device_id_type=mesh_id,
    )
    to_next.start()

    node = lax.rem(lane, 64)
    for c in range(3):
        mortar_pad[c, 8:136, :] = sums[c]
    for c in range(3):
        above = mortar_pad[c, 9:137, :]
        below = mortar_pad[c, 7:135, :]
        shared = (
            sums[c]
            + jnp.where(node >= 56, pltpu.roll(above, 56, 1), 0.0)
            + jnp.where(node < 8, pltpu.roll(below, 72, 1), 0.0)
        )
        flipped = pltpu.roll(shared, 64, 1)
        pair = side_by_side(shared)
        slopes = mm(pair, late[:, FORWARD : FORWARD + 256]) + mm(
            pair, late[:, FORWARD + 256 : FORWARD + 512]
        )
        for g in range(2 if c < 2 else 1):
            f = 2 * c + g
            twice = jnp.where(left == (g == 0), shared, flipped)
            inner = face_met[...] * slopes[:, 128 * g : 128 * g + 128] + face_vel[...] * twice
            inner = side_by_side(inner)
            for n, cols in enumerate(HALF):
                at = 256 * n
                everywhere = mm(pair, late[:, EXPAND + 512 * g + at : EXPAND + 512 * g + at + 256])
                low_face = mm(inner, late[:, DOWN + at : DOWN + at + 256]) + mm(
                    inner, late[:, DOWN + 512 + at : DOWN + 512 + at + 256]
                )
                out_ref[f, :, cols] = out_ref[f, :, cols] + everywhere * w_ref[:, cols] + low_face

    to_prev.wait_recv()
    to_next.wait_recv()
    has_next = jnp.where(place < total - 1, 1.0, 0.0)
    has_prev = jnp.where(place > 0, 1.0, 0.0)
    from_next = edge_got[0] * has_next
    from_prev = edge_got[1] * has_prev
    face = jnp.concatenate(
        [
            jnp.where(left[:8], pltpu.roll(from_prev, 64, 1), from_prev),
            jnp.where(left[:8], from_next, pltpu.roll(from_next, 64, 1)),
        ],
        axis=0,
    )
    slope = mm(side_by_side(face), late[:, SINGLE : SINGLE + 128])
    inner = side_by_side(edge_met[...] * slope + edge_vel[...] * face)
    back = mm(inner, late[:, SINGLE_BACK : SINGLE_BACK + 128]) + mm(
        inner, late[:, SINGLE_BACK + 128 : SINGLE_BACK + 256]
    )
    part = jnp.concatenate([face] * 4, axis=1) * wi_ref[...]
    part = part + jnp.concatenate(
        [
            jnp.where(head16 & left16, back, 0.0),
            jnp.zeros((16, 256), F32),
            jnp.where(head16 | left16, 0.0, back),
        ],
        axis=1,
    )
    for f in range(5):
        out_ref[f, 0:1, :] = out_ref[f, 0:1, :] + part[f : f + 1, :]
        out_ref[f, 127:128, :] = out_ref[f, 127:128, :] + part[8 + f : 9 + f, :]

    for copy in copies:
        copy.wait_send()
    to_prev.wait_send()
    to_next.wait_send()


def shards(n_dom, n_sub, adjoint_field, metric, velocity, route, element, code, hanging):
    fields = [jnp.transpose(a, (1, 0, 2)) for a in (adjoint_field, metric, velocity)]
    rows = [a.reshape(1, 128) for a in (route, element, code, hanging)]
    consts = [jnp.asarray(t) for t in tables()]
    operands = [pltpu.with_memory_space_constraint(a, pltpu.HBM) for a in fields + rows + consts]
    result = pl.pallas_call(
        functools.partial(kernel, n_dom, n_sub),
        out_shape=pltpu.VMEM((5, 128, 512), F32),
        in_specs=[pl.BlockSpec(memory_space=pltpu.HBM)] * len(operands),
        out_specs=pl.BlockSpec(memory_space=pltpu.VMEM),
        scratch_shapes=[pltpu.VMEM(a.shape, a.dtype) for a in operands]
        + [
            pltpu.VMEM((ROWS, 128), BF),
            pltpu.VMEM((4, ROWS, 128), BF),
            pltpu.VMEM((8, 128), F32),
            pltpu.VMEM((8, 128), F32),
            pltpu.VMEM((2, 8, 128), F32),
            pltpu.VMEM((5, 144, 128), F32),
            pltpu.VMEM((5, 144, 128), F32),
            pltpu.VMEM((3, 144, 128), F32),
            pltpu.VMEM((128, 512), F32),
            pltpu.VMEM((128, 128), F32),
            pltpu.VMEM((128, 128), F32),
            pltpu.VMEM((16, 512), F32),
            pltpu.VMEM((16, 128), F32),
            pltpu.VMEM((16, 128), F32),
            pltpu.SemaphoreType.DMA((13,)),
            pltpu.SemaphoreType.DMA((4,)),
            pltpu.SemaphoreType.DMA((4,)),
            pltpu.SemaphoreType.DMA((2,)),
            pltpu.SemaphoreType.DMA((2,)),
        ],
        compiler_params=pltpu.CompilerParams(
            collective_id=0, has_side_effects=True, vmem_limit_bytes=40 << 20
        ),
        name="adjoint",
    )(*operands)
    return jnp.transpose(result, (1, 0, 2))


def solution(mesh):
    sizes = dict(zip(mesh.axis_names, mesh.devices.shape))
    block = P(("dom", "sub"), None, None)
    flat = P(("dom", "sub"), None)
    return jax.shard_map(
        functools.partial(shards, sizes["dom"], sizes["sub"]),
        mesh=mesh,
        in_specs=(block, block, block, flat, flat, flat, flat),
        out_specs=block,
        check_vma=False,
    )
```

time: 40.7 us -> 30 us (0.74)
  local copies, waits for them, and re-layouts: 6.87 us -> 1.06 us
  Pallas kernels: 33.4 us -> 28.8 us
    unnamed x24 -> x1, local copies, waits for them, and re-layouts: 6.87 us -> 1.06 us
    pallas_call x2 -> x1, Pallas kernels: 33.4 us -> 28.8 us  [shards(): pl.pallas_call(functools.partial(kernel, n_dom, n_sub), out_shape=pltpu.V...]
where the time goes in v2:
time: 30 us; the launch traced here: 29.9 us
  Pallas kernels  28.8 us (96%)
  local copies, waits for them, and re-layouts  1.06 us (4%)
    pallas_call x1, Pallas kernels, shards(): pl.pallas_call(functools.partial(kernel, n_dom, n_sub), out_shape=pltpu.V...  28.8 us
    unnamed x1, local copies, waits for them, and re-layouts  1.06 us

profile of v2, /device:TPU:1, one launch (start us, length us, event | category | flops | bytes accessed | tf_op | source)
XLA Modules:
  0.0 29.9 jit_solution(16327348851767811686)
XLA Ops:
  0.0 28.8 %adjoint.1 = f32[5,128,512]{2,1,0:T(8,128)S(1)} custom-call(f32[5,128,512]{2,1,0:T(8,128)} %bitcast.9, f32[3,128,512]{2,1,0:T(8,128)} %bitcast.10, f32[3,128,512]{2,1,0:T(8,128)} %bitcast.11, s32[1,128]{1,0:T(1,128)} %bitcast.12, s32[1,128]{1,0:T(1,128)} %bitcast.13, s32[1,128]{1,0:T(1,128)} %bitcast.14, s32[1,128]{1,0:T(1,128)} %bitcast.15, ...), custom_call_target="tpu_custom_call" | custom-call | tf_op jit(solution)/shard_map/adjoint/pallas_call | solution.py:548
  28.8 1.1 %copy.15 = f32[128,5,512]{2,0,1:T(8,128)} copy(f32[128,5,512]{2,0,1:T(8,128)S(1)} %bitcast.8) | data formatting | bytes 2621440

commit v3 on v2

--- a/solution.py
+++ b/solution.py
@@ -228,7 +228,7 @@
     out_ref = refs[13]
     (x, met, vel, route_ref, elem_ref, code_ref, hang_ref) = refs[14:21]
     (fold, i_tab, jk_tab, pick, late, vecs) = refs[21:27]
-    (send, got, low_send, high_send, edge_got, low_pad, high_pad, mortar_pad) = refs[27:35]
+    (send, got, edge_send, edge_got, edge_face, low_pad, high_pad, mortar_pad) = refs[27:35]
     (w_ref, face_met, face_vel, wi_ref, edge_met, edge_vel) = refs[35:41]
     (load_sem, send_sem, recv_sem, edge_send_sem, edge_recv_sem) = refs[41:46]
 
@@ -238,10 +238,13 @@
     peers = [{"dom": lax.rem(dom + o + n_dom, n_dom), "sub": sub} for o in OFFSETS]
     place = dom * n_sub + sub
     total = n_dom * n_sub
-    before = lax.rem(place + total - 1, total)
-    after = lax.rem(place + 1, total)
-    prev_dev = {"dom": before // n_sub, "sub": lax.rem(before, n_sub)}
-    next_dev = {"dom": after // n_sub, "sub": lax.rem(after, n_sub)}
+
+    def stepped(offset, step):
+        at = lax.rem(dom + offset + n_dom, n_dom) * n_sub + sub
+        at = lax.rem(at + step + total, total)
+        return {"dom": at // n_sub, "sub": lax.rem(at, n_sub)}
+
+    edge_peers = [stepped(o, 1) for o in range(-2, 3)] + [stepped(o, -1) for o in range(-2, 3)]
 
     loads = []
 
@@ -251,7 +254,7 @@
         loads.append(copy)
         return copy
 
-    x_loads = [load(x_hbm, x)]
+    x_loads = []
     first_loads = [
         load(fold_hbm, fold),
         load(code_hbm, code_ref),
@@ -259,8 +262,10 @@
         load(route_hbm, route_ref),
         load(elem_hbm, elem_ref),
     ]
+    for f in range(5):
+        x_loads.append(load(x_hbm.at[f], x.at[f]))
     barrier = pltpu.get_barrier_semaphore()
-    for dev in peers + [prev_dev, next_dev]:
+    for dev in peers + edge_peers:
         pl.semaphore_signal(barrier, inc=1, device_id=dev, device_id_type=mesh_id)
     later_loads = [
         load(i_hbm, i_tab),
@@ -277,11 +282,10 @@
     left = lane < 64
     slot = lax.rem(lane, 64) // 8
 
-    low_send[...] = jnp.zeros((8, 128), F32)
-    high_send[...] = jnp.zeros((8, 128), F32)
     for f in range(5):
         low_pad[f, 136:144, :] = jnp.zeros((8, 128), F32)
         high_pad[f, 0:8, :] = jnp.zeros((8, 128), F32)
+    edge_face[...] = jnp.zeros((2, 8, 128), F32)
     for c in range(3):
         mortar_pad[c, 0:8, :] = jnp.zeros((8, 128), F32)
         mortar_pad[c, 136:144, :] = jnp.zeros((8, 128), F32)
@@ -296,10 +300,10 @@
     hang = column(hang_ref)
     odd = lax.rem(code, 2) == 1
 
-    for copy in x_loads:
-        copy.wait()
+    keep = jnp.where(slot == 7, 1.0 - hang, 1.0)
     faces = []
     for f in range(5):
+        x_loads[f].wait()
         packed = jnp.where(
             slot == 7,
             x[f, :, 0:128],
@@ -325,8 +329,29 @@
         picked = picked * hang
         other = pltpu.roll(picked, 64, 1)
         faces.append((jnp.where(odd, other, picked), jnp.where(odd, picked, other)))
-    send[0:128, :] = jnp.where(left, faces[0][0], faces[1][1]).astype(BF)
-    send[128:256, :] = jnp.where(left, faces[2][0], faces[3][1]).astype(BF)
+    pairs = [
+        jnp.where(left, faces[0][0], faces[1][1]).astype(BF),
+        jnp.where(left, faces[2][0], faces[3][1]).astype(BF),
+        faces[4][0].astype(BF),
+    ]
+    edge_row = lax.broadcasted_iota(jnp.int32, (80, 128), 0)
+    tile = edge_row // 8
+    part = lax.rem(edge_row, 8)
+    wanted_elem = jnp.where(tile < 5, 127, 0)
+    wanted_dom = lax.rem(dom + lax.rem(tile, 5) - 2 + n_dom, n_dom)
+    chosen = (jnp.broadcast_to(route_ref[...], (80, 128)) == wanted_dom) & (
+        jnp.broadcast_to(elem_ref[...], (80, 128)) == wanted_elem
+    )
+    chosen = jnp.where(chosen, 1.0, 0.0)
+    edge_sums = jnp.zeros((80, 128), F32)
+    for c in range(3):
+        edge_sums += mm(jnp.where(part == c, chosen, 0.0).astype(BF), pairs[c])
+    edge_send[...] = edge_sums
+    for f in range(5):
+        edge_send[19 + f : 20 + f, :] = x[f, 127:128, 384:512] * keep[127:128, :]
+        edge_send[59 + f : 60 + f, :] = x[f, 0:1, 0:128] * keep[0:1, :]
+    send[0:128, :] = pairs[0]
+    send[128:256, :] = pairs[1]
     send[256:320, :] = jnp.where(left[:64], faces[4][0][:64], faces[4][1][64:]).astype(BF)
     meta_row = lax.broadcasted_iota(jnp.int32, (16, 128), 0)
     send[320:336, :] = jnp.where(
@@ -335,7 +360,20 @@
         jnp.broadcast_to(elem_ref[...].astype(F32), (16, 128)),
     ).astype(BF)
 
-    pl.semaphore_wait(barrier, 6)
+    pl.semaphore_wait(barrier, 14)
+    edge_copies = []
+    for n, dev in enumerate(edge_peers):
+        rows = pl.ds(8 * n, 8)
+        copy = pltpu.make_async_remote_copy(
+            src_ref=edge_send.at[rows],
+            dst_ref=edge_got.at[rows],
+            send_sem=edge_send_sem.at[n],
+            recv_sem=edge_recv_sem.at[n],
+            device_id=dev,
+            device_id_type=mesh_id,
+        )
+        copy.start()
+        edge_copies.append(copy)
     copies = []
     for n, dev in enumerate(peers):
         copy = pltpu.make_async_remote_copy(
@@ -349,8 +387,6 @@
         copy.start()
         copies.append(copy)
 
-    keep = 1.0 - hang
-    keep = jnp.where(slot == 7, keep, 1.0)
     for f in range(5):
         x[f, :, 128:256] = x[f, :, 128:256] * keep
         x[f, :, 256:384] = x[f, :, 256:384] * keep
@@ -443,37 +479,6 @@
         sums = absorb(sums, got.at[n])
     sums[2] = sums[2] + pltpu.roll(sums[2], 64, 1)
 
-    lane8 = lane[:8]
-    for f in range(5):
-        part = sums[f // 2]
-        top, bottom = part[0:8, :], part[120:128, :]
-        shift_low, shift_high = (64, 72) if f % 2 else (0, 8)
-        if shift_low:
-            top = pltpu.roll(top, shift_low, 1)
-        bottom = pltpu.roll(bottom, shift_high, 1)
-        top = jnp.where(lane8 < 8, top, 0.0)
-        bottom = jnp.where((lane8 >= 64) & (lane8 < 72), bottom, 0.0)
-        low_send[f : f + 1, :] = low_pad[f, 8:9, :] + top[0:1, :]
-        high_send[f : f + 1, :] = high_pad[f, 135:136, :] + bottom[7:8, :]
-    to_prev = pltpu.make_async_remote_copy(
-        src_ref=low_send,
-        dst_ref=edge_got.at[0],
-        send_sem=edge_send_sem.at[0],
-        recv_sem=edge_recv_sem.at[0],
-        device_id=prev_dev,
-        device_id_type=mesh_id,
-    )
-    to_prev.start()
-    to_next = pltpu.make_async_remote_copy(
-        src_ref=high_send,
-        dst_ref=edge_got.at[1],
-        send_sem=edge_send_sem.at[1],
-        recv_sem=edge_recv_sem.at[1],
-        device_id=next_dev,
-        device_id_type=mesh_id,
-    )
-    to_next.start()
-
     node = lax.rem(lane, 64)
     for c in range(3):
         mortar_pad[c, 8:136, :] = sums[c]
@@ -503,12 +508,24 @@
                 )
                 out_ref[f, :, cols] = out_ref[f, :, cols] + everywhere * w_ref[:, cols] + low_face
 
-    to_prev.wait_recv()
-    to_next.wait_recv()
+    for copy in edge_copies:
+        copy.wait_recv()
+    tiles = [edge_got[8 * n : 8 * n + 8, :] for n in range(10)]
+    high_tile = tiles[0] + tiles[1] + tiles[2] + tiles[3] + tiles[4]
+    low_tile = tiles[5] + tiles[6] + tiles[7] + tiles[8] + tiles[9]
+    lane8 = lane[:8]
+    at_high = (lane8 >= 64) & (lane8 < 72)
+    at_low = lane8 < 8
+    highs = [jnp.where(at_high, pltpu.roll(high_tile, n, 1), 0.0) for n in (8, 72)]
+    lows = [jnp.where(at_low, low_tile, 0.0), jnp.where(at_low, pltpu.roll(low_tile, 64, 1), 0.0)]
+    for f in range(5):
+        c, g = divmod(f, 2)
+        edge_face[0, f : f + 1, :] = high_tile[3 + f : 4 + f, :] + highs[g][c : c + 1, :]
+        edge_face[1, f : f + 1, :] = low_tile[3 + f : 4 + f, :] + lows[g][c : c + 1, :]
     has_next = jnp.where(place < total - 1, 1.0, 0.0)
     has_prev = jnp.where(place > 0, 1.0, 0.0)
-    from_next = edge_got[0] * has_next
-    from_prev = edge_got[1] * has_prev
+    from_prev = edge_face[0] * has_prev
+    from_next = edge_face[1] * has_next
     face = jnp.concatenate(
         [
             jnp.where(left[:8], pltpu.roll(from_prev, 64, 1), from_prev),
@@ -536,8 +553,8 @@
 
     for copy in copies:
         copy.wait_send()
-    to_prev.wait_send()
-    to_next.wait_send()
+    for copy in edge_copies:
+        copy.wait_send()
 
 
 def shards(n_dom, n_sub, adjoint_field, metric, velocity, route, element, code, hanging):
@@ -554,8 +571,8 @@
         + [
             pltpu.VMEM((ROWS, 128), BF),
             pltpu.VMEM((4, ROWS, 128), BF),
-            pltpu.VMEM((8, 128), F32),
-            pltpu.VMEM((8, 128), F32),
+            pltpu.VMEM((80, 128), F32),
+            pltpu.VMEM((80, 128), F32),
             pltpu.VMEM((2, 8, 128), F32),
             pltpu.VMEM((5, 144, 128), F32),
             pltpu.VMEM((5, 144, 128), F32),
@@ -566,11 +583,11 @@
             pltpu.VMEM((16, 512), F32),
             pltpu.VMEM((16, 128), F32),
             pltpu.VMEM((16, 128), F32),
-            pltpu.SemaphoreType.DMA((13,)),
+            pltpu.SemaphoreType.DMA((17,)),
             pltpu.SemaphoreType.DMA((4,)),
             pltpu.SemaphoreType.DMA((4,)),
-            pltpu.SemaphoreType.DMA((2,)),
-            pltpu.SemaphoreType.DMA((2,)),
+            pltpu.SemaphoreType.DMA((10,)),
+            pltpu.SemaphoreType.DMA((10,)),
         ],
         compiler_params=pltpu.CompilerParams(
             collective_id=0, has_side_effects=True, vmem_limit_bytes=40 << 20

time: 30 us -> 29.3 us (0.977)
  Pallas kernels: 28.8 us -> 28.1 us
    pallas_call x1, Pallas kernels: 28.8 us -> 28.1 us  [shards(): pl.pallas_call(functools.partial(kernel, n_dom, n_sub), out_shape=pltpu.V...]
where the time goes in v3:
time: 29.3 us; the launch traced here: 29.2 us
  Pallas kernels  28.1 us (96%)
  local copies, waits for them, and re-layouts  1.06 us (4%)
    pallas_call x1, Pallas kernels, shards(): pl.pallas_call(functools.partial(kernel, n_dom, n_sub), out_shape=pltpu.V...  28.1 us
    unnamed x1, local copies, waits for them, and re-layouts  1.06 us

profile of v3, /device:TPU:1, one launch (start us, length us, event | category | flops | bytes accessed | tf_op | source)
XLA Modules:
  0.0 29.2 jit_solution(5804801223074071952)
XLA Ops:
  0.0 28.1 %adjoint.1 = f32[5,128,512]{2,1,0:T(8,128)S(1)} custom-call(f32[5,128,512]{2,1,0:T(8,128)} %bitcast.9, f32[3,128,512]{2,1,0:T(8,128)} %bitcast.10, f32[3,128,512]{2,1,0:T(8,128)} %bitcast.11, s32[1,128]{1,0:T(1,128)} %bitcast.12, s32[1,128]{1,0:T(1,128)} %bitcast.13, s32[1,128]{1,0:T(1,128)} %bitcast.14, s32[1,128]{1,0:T(1,128)} %bitcast.15, ...), custom_call_target="tpu_custom_call" | custom-call | tf_op jit(solution)/shard_map/adjoint/pallas_call | solution.py:565
  28.1 1.1 %copy.15 = f32[128,5,512]{2,0,1:T(8,128)} copy(f32[128,5,512]{2,0,1:T(8,128)S(1)} %bitcast.8) | data formatting | bytes 2621440

commit v4 on v3

--- a/solution.py
+++ b/solution.py
@@ -225,26 +225,32 @@
 def kernel(n_dom, n_sub, *refs):
     (x_hbm, met_hbm, vel_hbm, route_hbm, elem_hbm, code_hbm, hang_hbm) = refs[:7]
     (fold_hbm, i_hbm, jk_hbm, pick_hbm, late_hbm, vecs_hbm) = refs[7:13]
-    out_ref = refs[13]
-    (x, met, vel, route_ref, elem_ref, code_ref, hang_ref) = refs[14:21]
-    (fold, i_tab, jk_tab, pick, late, vecs) = refs[21:27]
-    (send, got, edge_send, edge_got, edge_face, low_pad, high_pad, mortar_pad) = refs[27:35]
-    (w_ref, face_met, face_vel, wi_ref, edge_met, edge_vel) = refs[35:41]
-    (load_sem, send_sem, recv_sem, edge_send_sem, edge_recv_sem) = refs[41:46]
+    (out_ref, shared_ref, ends_ref, w_ref, face_met, face_vel, late) = refs[13:20]
+    (x, met, vel, route_ref, elem_ref, code_ref, hang_ref) = refs[20:27]
+    (fold, i_tab, jk_tab, pick, vecs) = refs[27:32]
+    (send, got, edge_send, edge_got, edge_face, low_pad, high_pad, mortar_pad) = refs[32:40]
+    (wi_ref, edge_met, edge_vel) = refs[40:43]
+    (load_sem, send_sem, recv_sem, edge_send_sem, edge_recv_sem) = refs[43:48]
 
     dom = lax.axis_index("dom")
     sub = lax.axis_index("sub")
     mesh_id = pl.DeviceIdType.MESH
-    peers = [{"dom": lax.rem(dom + o + n_dom, n_dom), "sub": sub} for o in OFFSETS]
     place = dom * n_sub + sub
     total = n_dom * n_sub
 
-    def stepped(offset, step):
-        at = lax.rem(dom + offset + n_dom, n_dom) * n_sub + sub
-        at = lax.rem(at + step + total, total)
-        return {"dom": at // n_sub, "sub": lax.rem(at, n_sub)}
-
-    edge_peers = [stepped(o, 1) for o in range(-2, 3)] + [stepped(o, -1) for o in range(-2, 3)]
+    def along(offset):
+        at = dom + offset
+        at = jnp.where(at < 0, at + n_dom, at)
+        return jnp.where(at >= n_dom, at - n_dom, at)
+
+    peers = [{"dom": along(o), "sub": sub} for o in OFFSETS]
+    last, first = sub == n_sub - 1, sub == 0
+    sub_up = jnp.where(last, 0, sub + 1)
+    sub_down = jnp.where(first, n_sub - 1, sub - 1)
+    dom_up = jnp.where(last, 1, 0)
+    dom_down = jnp.where(first, -1, 0)
+    edge_peers = [{"dom": along(o + dom_up), "sub": sub_up} for o in range(-2, 3)]
+    edge_peers += [{"dom": along(o + dom_down), "sub": sub_down} for o in range(-2, 3)]
 
     loads = []
 
@@ -254,19 +260,44 @@
         loads.append(copy)
         return copy
 
-    x_loads = []
+    x_loads = [load(x_hbm.at[f], x.at[f]) for f in range(5)]
     first_loads = [
-        load(fold_hbm, fold),
         load(code_hbm, code_ref),
         load(hang_hbm, hang_ref),
         load(route_hbm, route_ref),
         load(elem_hbm, elem_ref),
+        load(fold_hbm, fold),
     ]
-    for f in range(5):
-        x_loads.append(load(x_hbm.at[f], x.at[f]))
     barrier = pltpu.get_barrier_semaphore()
     for dev in peers + edge_peers:
         pl.semaphore_signal(barrier, inc=1, device_id=dev, device_id_type=mesh_id)
+
+    lane = lax.broadcasted_iota(jnp.int32, (128, 128), 1)
+    row = lax.broadcasted_iota(jnp.int32, (128, 128), 0)
+    left = lane < 64
+    slot = lax.rem(lane, 64) // 8
+
+    for f in range(5):
+        low_pad[f, 136:144, :] = jnp.zeros((8, 128), F32)
+        high_pad[f, 0:8, :] = jnp.zeros((8, 128), F32)
+    edge_face[...] = jnp.zeros((2, 8, 128), F32)
+    for c in range(3):
+        mortar_pad[c, 0:8, :] = jnp.zeros((8, 128), F32)
+        mortar_pad[c, 136:144, :] = jnp.zeros((8, 128), F32)
+
+    for copy in first_loads:
+        copy.wait()
+
+    def column(ref):
+        return jnp.broadcast_to(ref[...].astype(F32), (128, 128)).T
+
+    code = column(code_ref).astype(jnp.int32)
+    hang = column(hang_ref)
+    odd = lax.rem(code, 2) == 1
+
+    keep = jnp.where(slot == 7, 1.0 - hang, 1.0)
+    for copy in x_loads:
+        copy.wait()
     later_loads = [
         load(i_hbm, i_tab),
         load(jk_hbm, jk_tab),
@@ -276,34 +307,8 @@
         load(late_hbm, late),
         load(vecs_hbm, vecs),
     ]
-
-    lane = lax.broadcasted_iota(jnp.int32, (128, 128), 1)
-    row = lax.broadcasted_iota(jnp.int32, (128, 128), 0)
-    left = lane < 64
-    slot = lax.rem(lane, 64) // 8
-
-    for f in range(5):
-        low_pad[f, 136:144, :] = jnp.zeros((8, 128), F32)
-        high_pad[f, 0:8, :] = jnp.zeros((8, 128), F32)
-    edge_face[...] = jnp.zeros((2, 8, 128), F32)
-    for c in range(3):
-        mortar_pad[c, 0:8, :] = jnp.zeros((8, 128), F32)
-        mortar_pad[c, 136:144, :] = jnp.zeros((8, 128), F32)
-
-    for copy in first_loads:
-        copy.wait()
-
-    def column(ref):
-        return jnp.broadcast_to(ref[...].astype(F32), (128, 128)).T
-
-    code = column(code_ref).astype(jnp.int32)
-    hang = column(hang_ref)
-    odd = lax.rem(code, 2) == 1
-
-    keep = jnp.where(slot == 7, 1.0 - hang, 1.0)
-    faces = []
-    for f in range(5):
-        x_loads[f].wait()
+    lefts = []
+    for f in range(5):
         packed = jnp.where(
             slot == 7,
             x[f, :, 0:128],
@@ -320,11 +325,15 @@
         high = packed.astype(BF)
         low = packed - high.astype(F32)
         mixed = jnp.where(slot >= 4, packed, pltpu.roll(low, 96, 1)).astype(BF)
-        mapped = mm(jnp.concatenate([mixed, high], axis=1), fold[...])
+        lefts.append(jnp.concatenate([mixed, high], axis=1))
+    mapped = mm(jnp.concatenate(lefts, axis=0), fold[...])
+    faces = []
+    for f in range(5):
+        one = mapped[128 * f : 128 * f + 128]
         picked = jnp.where(
             code < 4,
-            jnp.where(code < 2, mapped[:, 0:128], mapped[:, 128:256]),
-            jnp.where(code < 6, mapped[:, 256:384], mapped[:, 384:512]),
+            jnp.where(code < 2, one[:, 0:128], one[:, 128:256]),
+            jnp.where(code < 6, one[:, 256:384], one[:, 384:512]),
         )
         picked = picked * hang
         other = pltpu.roll(picked, 64, 1)
@@ -361,31 +370,39 @@
     ).astype(BF)
 
     pl.semaphore_wait(barrier, 14)
-    edge_copies = []
-    for n, dev in enumerate(edge_peers):
+    edge_copies, copies = [None] * 10, [None] * 4
+
+    def send_edge(n):
         rows = pl.ds(8 * n, 8)
-        copy = pltpu.make_async_remote_copy(
+        edge_copies[n] = pltpu.make_async_remote_copy(
             src_ref=edge_send.at[rows],
             dst_ref=edge_got.at[rows],
             send_sem=edge_send_sem.at[n],
             recv_sem=edge_recv_sem.at[n],
-            device_id=dev,
+            device_id=edge_peers[n],
             device_id_type=mesh_id,
         )
-        copy.start()
-        edge_copies.append(copy)
-    copies = []
-    for n, dev in enumerate(peers):
-        copy = pltpu.make_async_remote_copy(
+        edge_copies[n].start()
+
+    def send_faces(n):
+        copies[n] = pltpu.make_async_remote_copy(
             src_ref=send,
             dst_ref=got.at[n],
             send_sem=send_sem.at[n],
             recv_sem=recv_sem.at[n],
-            device_id=dev,
+            device_id=peers[n],
             device_id_type=mesh_id,
         )
-        copy.start()
-        copies.append(copy)
+        copies[n].start()
+
+    for n in (4, 9, 3, 8):
+        send_edge(n)
+    send_faces(3)
+    send_faces(2)
+    for n in (2, 7, 1, 6, 0, 5):
+        send_edge(n)
+    send_faces(1)
+    send_faces(0)
 
     for f in range(5):
         x[f, :, 128:256] = x[f, :, 128:256] * keep
@@ -474,8 +491,8 @@
         ]
 
     sums = absorb([jnp.zeros((128, 128), F32)] * 3, send)
-    for n, copy in enumerate(copies):
-        copy.wait_recv()
+    for n in (0, 1, 2, 3):
+        copies[n].wait_recv()
         sums = absorb(sums, got.at[n])
     sums[2] = sums[2] + pltpu.roll(sums[2], 64, 1)
 
@@ -485,28 +502,11 @@
     for c in range(3):
         above = mortar_pad[c, 9:137, :]
         below = mortar_pad[c, 7:135, :]
-        shared = (
+        shared_ref[c] = (
             sums[c]
             + jnp.where(node >= 56, pltpu.roll(above, 56, 1), 0.0)
             + jnp.where(node < 8, pltpu.roll(below, 72, 1), 0.0)
         )
-        flipped = pltpu.roll(shared, 64, 1)
-        pair = side_by_side(shared)
-        slopes = mm(pair, late[:, FORWARD : FORWARD + 256]) + mm(
-            pair, late[:, FORWARD + 256 : FORWARD + 512]
-        )
-        for g in range(2 if c < 2 else 1):
-            f = 2 * c + g
-            twice = jnp.where(left == (g == 0), shared, flipped)
-            inner = face_met[...] * slopes[:, 128 * g : 128 * g + 128] + face_vel[...] * twice
-            inner = side_by_side(inner)
-            for n, cols in enumerate(HALF):
-                at = 256 * n
-                everywhere = mm(pair, late[:, EXPAND + 512 * g + at : EXPAND + 512 * g + at + 256])
-                low_face = mm(inner, late[:, DOWN + at : DOWN + at + 256]) + mm(
-                    inner, late[:, DOWN + 512 + at : DOWN + 512 + at + 256]
-                )
-                out_ref[f, :, cols] = out_ref[f, :, cols] + everywhere * w_ref[:, cols] + low_face
 
     for copy in edge_copies:
         copy.wait_recv()
@@ -547,14 +547,51 @@
         ],
         axis=1,
     )
-    for f in range(5):
-        out_ref[f, 0:1, :] = out_ref[f, 0:1, :] + part[f : f + 1, :]
-        out_ref[f, 127:128, :] = out_ref[f, 127:128, :] + part[8 + f : 9 + f, :]
+    ends_ref[...] = part
 
     for copy in copies:
         copy.wait_send()
     for copy in edge_copies:
         copy.wait_send()
+
+
+def finish_kernel(local, shared_ref, ends_ref, w_ref, face_met, face_vel, late, out_hbm, res, sem):
+    left = lax.broadcasted_iota(jnp.int32, (128, 128), 1) < 64
+    shared = [shared_ref[c] for c in range(3)]
+    pairs = jnp.concatenate([side_by_side(part) for part in shared], axis=0)
+    slopes = mm(pairs, late[:, FORWARD : FORWARD + 256]) + mm(
+        pairs, late[:, FORWARD + 256 : FORWARD + 512]
+    )
+    inners = []
+    for f in range(5):
+        c, g = divmod(f, 2)
+        twice = jnp.where(left == (g == 0), shared[c], pltpu.roll(shared[c], 64, 1))
+        slope = slopes[128 * c : 128 * c + 128, 128 * g : 128 * g + 128]
+        inners.append(side_by_side(face_met[...] * slope + face_vel[...] * twice))
+    inners = jnp.concatenate(inners, axis=0)
+    every, lows = [], []
+    for at in (0, 256):
+        even = mm(pairs, late[:, EXPAND + at : EXPAND + at + 256])
+        odd = mm(pairs[:256], late[:, EXPAND + 512 + at : EXPAND + 512 + at + 256])
+        every.append((even, odd))
+        lows.append(
+            mm(inners, late[:, DOWN + at : DOWN + at + 256])
+            + mm(inners, late[:, DOWN + 512 + at : DOWN + 512 + at + 256])
+        )
+    copies = []
+    for f in range(5):
+        c, g = divmod(f, 2)
+        for n, cols in enumerate(HALF):
+            spread = every[n][g][128 * c : 128 * c + 128]
+            low = lows[n][128 * f : 128 * f + 128]
+            res[f, :, cols] = local[f, :, cols] + spread * w_ref[:, cols] + low
+        res[f, 0:1, :] = res[f, 0:1, :] + ends_ref[f : f + 1, :]
+        res[f, 127:128, :] = res[f, 127:128, :] + ends_ref[8 + f : 9 + f, :]
+        copy = pltpu.make_async_copy(res.at[f], out_hbm.at[f], sem.at[f])
+        copy.start()
+        copies.append(copy)
+    for copy in copies:
+        copy.wait()
 
 
 def shards(n_dom, n_sub, adjoint_field, metric, velocity, route, element, code, hanging):
@@ -562,12 +599,22 @@
     rows = [a.reshape(1, 128) for a in (route, element, code, hanging)]
     consts = [jnp.asarray(t) for t in tables()]
     operands = [pltpu.with_memory_space_constraint(a, pltpu.HBM) for a in fields + rows + consts]
-    result = pl.pallas_call(
+    made = [
+        pltpu.VMEM((5, 128, 512), F32),
+        pltpu.VMEM((3, 128, 128), F32),
+        pltpu.VMEM((16, 512), F32),
+        pltpu.VMEM((128, 512), F32),
+        pltpu.VMEM((128, 128), F32),
+        pltpu.VMEM((128, 128), F32),
+        pltpu.VMEM(consts[4].shape, BF),
+    ]
+    held = fields + rows + consts[:4] + consts[5:]
+    handed = pl.pallas_call(
         functools.partial(kernel, n_dom, n_sub),
-        out_shape=pltpu.VMEM((5, 128, 512), F32),
+        out_shape=made,
         in_specs=[pl.BlockSpec(memory_space=pltpu.HBM)] * len(operands),
-        out_specs=pl.BlockSpec(memory_space=pltpu.VMEM),
-        scratch_shapes=[pltpu.VMEM(a.shape, a.dtype) for a in operands]
+        out_specs=[pl.BlockSpec(memory_space=pltpu.VMEM)] * len(made),
+        scratch_shapes=[pltpu.VMEM(a.shape, a.dtype) for a in held]
         + [
             pltpu.VMEM((ROWS, 128), BF),
             pltpu.VMEM((4, ROWS, 128), BF),
@@ -577,9 +624,6 @@
             pltpu.VMEM((5, 144, 128), F32),
             pltpu.VMEM((5, 144, 128), F32),
             pltpu.VMEM((3, 144, 128), F32),
-            pltpu.VMEM((128, 512), F32),
-            pltpu.VMEM((128, 128), F32),
-            pltpu.VMEM((128, 128), F32),
             pltpu.VMEM((16, 512), F32),
             pltpu.VMEM((16, 128), F32),
             pltpu.VMEM((16, 128), F32),
@@ -594,6 +638,16 @@
         ),
         name="adjoint",
     )(*operands)
+    handed = [pltpu.with_memory_space_constraint(a, pltpu.VMEM) for a in handed]
+    result = pl.pallas_call(
+        finish_kernel,
+        out_shape=jax.ShapeDtypeStruct((5, 128, 512), F32),
+        in_specs=[pl.BlockSpec(memory_space=pltpu.VMEM)] * len(handed),
+        out_specs=pl.BlockSpec(memory_space=pltpu.HBM),
+        scratch_shapes=[pltpu.VMEM((5, 128, 512), F32), pltpu.SemaphoreType.DMA((5,))],
+        compiler_params=pltpu.CompilerParams(vmem_limit_bytes=32 << 20),
+        name="finish",
+    )(*handed)
     return jnp.transpose(result, (1, 0, 2))
 
 

time: 29.3 us -> 29.1 us (level)
  local copies, waits for them, and re-layouts: 1.06 us -> 0 us
  Pallas kernels: 28.1 us -> 28.9 us
    unnamed x1 -> x0, local copies, waits for them, and re-layouts: 1.06 us -> none
    pallas_call x1 -> x2, Pallas kernels: 28.1 us -> 28.9 us  [the longest x1 27.2 us: shards(): pl.pallas_call(functools.partial(kernel, n_dom, n_sub), out_shape=made, i...]
where the time goes in v4:
time: 29.1 us; the launch traced here: 28.9 us
  Pallas kernels  28.9 us (99%)
    pallas_call x1, Pallas kernels, shards(): pl.pallas_call(functools.partial(kernel, n_dom, n_sub), out_shape=made, i...  27.2 us
    pallas_call x1, Pallas kernels, shards(): pl.pallas_call(finish_kernel, out_shape=jax.ShapeDtypeStruct((5, 128, 512...  1.75 us

profile of v4, /device:TPU:1, one launch (start us, length us, event | category | flops | bytes accessed | tf_op | source)
XLA Modules:
  0.0 28.9 jit_solution(5640087123263436298)
XLA Ops:
  0.0 27.2 %adjoint.1 = (f32[5,128,512]{2,1,0:T(8,128)S(1)}, f32[3,128,128]{2,1,0:T(8,128)S(1)}, f32[16,512]{1,0:T(8,128)S(1)}, f32[128,512]{1,0:T(8,128)S(1)}, f32[128,128...) custom-call(f32[5,128,512]{2,1,0:T(8,128)} %bitcast.8, f32[3,128,512]{2,1,0:T(8,128)} %bitcast.9, ...), custom_call_target="tpu_custom_call" | custom-call | tf_op jit(solution)/shard_map/adjoint/pallas_call | solution.py:612
  27.2 1.8 %finish.1 = f32[5,128,512]{2,1,0:T(8,128)} custom-call(f32[5,128,512]{2,1,0:T(8,128)S(1)} %get-tuple-element.12.local, f32[3,128,128]{2,1,0:T(8,128)S(1)} %get-tuple-element.13.shared_ref, f32[16,512]{1,0:T(8,128)S(1)} %get-tuple-element.14.ends_ref, f32[128,512]{1,0:T(8,128)S(1)} %get-tuple-element.15.w_ref, f32[128,128]{1,0:T(8,128)S(1)} %get-tuple-element.16.face_met, ...), custom_call_target="tpu_custom_call" | custom-call | tf_op jit(solution)/shard_map/finish/pallas_call | solution.py:642

commit v5 on v4

--- a/solution.py
+++ b/solution.py
@@ -369,12 +369,9 @@
         jnp.broadcast_to(elem_ref[...].astype(F32), (16, 128)),
     ).astype(BF)
 
-    pl.semaphore_wait(barrier, 14)
-    edge_copies, copies = [None] * 10, [None] * 4
-
-    def send_edge(n):
+    def edge_copy(n):
         rows = pl.ds(8 * n, 8)
-        edge_copies[n] = pltpu.make_async_remote_copy(
+        return pltpu.make_async_remote_copy(
             src_ref=edge_send.at[rows],
             dst_ref=edge_got.at[rows],
             send_sem=edge_send_sem.at[n],
@@ -382,10 +379,9 @@
             device_id=edge_peers[n],
             device_id_type=mesh_id,
         )
-        edge_copies[n].start()
-
-    def send_faces(n):
-        copies[n] = pltpu.make_async_remote_copy(
+
+    def face_copy(n):
+        return pltpu.make_async_remote_copy(
             src_ref=send,
             dst_ref=got.at[n],
             send_sem=send_sem.at[n],
@@ -393,87 +389,99 @@
             device_id=peers[n],
             device_id_type=mesh_id,
         )
-        copies[n].start()
-
-    for n in (4, 9, 3, 8):
-        send_edge(n)
-    send_faces(3)
-    send_faces(2)
-    for n in (2, 7, 1, 6, 0, 5):
-        send_edge(n)
-    send_faces(1)
-    send_faces(0)
-
-    for f in range(5):
-        x[f, :, 128:256] = x[f, :, 128:256] * keep
-        x[f, :, 256:384] = x[f, :, 256:384] * keep
-        low_pad[f, 8:136, :] = x[f, :, 0:128] * keep
-        high_pad[f, 8:136, :] = x[f, :, 384:512] * keep
-        above = low_pad[f, 9:137, :]
-        below = high_pad[f, 7:135, :]
-        x[f, :, 0:128] = low_pad[f, 8:136, :] + jnp.where(left, pltpu.roll(below, 64, 1), 0.0)
-        x[f, :, 384:512] = high_pad[f, 8:136, :] + jnp.where(left, 0.0, pltpu.roll(above, 64, 1))
-    for copy in later_loads:
-        copy.wait()
-    apply_operator(x, met, vel, i_tab, jk_tab, out_ref)
-
-    wide = lax.broadcasted_iota(jnp.int32, (128, 512), 1)
-    on_low = lax.rem(wide, 64) < 8
-    weight = met[1] * viscosity * vecs[0:1, :] + jnp.where(on_low, vel[1], 0.0)
-    wh, wl = halves_of(weight)
-    for cols in HALF:
-        w_ref[:, cols] = (
-            mmt(wh[:, cols], jk_tab[0, 0])
-            + mmt(wl[:, cols], jk_tab[0, 0])
-            + mmt(wh[:, cols], jk_tab[0, 1])
-        )
-
-    def low_nodes(src):
-        ah, al = halves_of(src[0])
-        bh, bl = halves_of(src[2])
-        return (
-            mm(ah, pick[:, 0:128])
-            + mm(al, pick[:, 0:128])
-            + mm(bh, pick[:, 128:256])
-            + mm(bl, pick[:, 128:256])
-        )
-
-    face_met[...] = low_nodes(met) * viscosity
-    face_vel[...] = low_nodes(vel)
-
-    edge_rows = lax.broadcasted_iota(jnp.int32, (16, 512), 0)
-    edge_wide = lax.broadcasted_iota(jnp.int32, (16, 512), 1)
-    head = edge_rows < 8
-
-    def ends(src, dim):
-        a = jnp.broadcast_to(src[dim, 0:1, :], (16, 512))
-        b = jnp.broadcast_to(src[dim, 127:128, :], (16, 512))
-        return a, b
-
-    ma, mb = ends(met, 0)
-    va, vb = ends(vel, 0)
-    ea = ma * viscosity * vecs[1:2, :] + jnp.where(edge_wide < 64, va, 0.0)
-    eb = mb * viscosity * vecs[2:3, :] + jnp.where(edge_wide >= 448, vb, 0.0)
-    eh, el = halves_of(jnp.where(head, ea, eb))
-    for cols in HALF:
-        acc = jnp.zeros((16, 256), F32)
-        for rows in HALF:
-            acc += mmt(eh[:, rows], i_tab[0, cols, rows])
-            acc += mmt(el[:, rows], i_tab[0, cols, rows])
-            acc += mmt(eh[:, rows], i_tab[1, cols, rows])
-        wi_ref[:, cols] = acc
+
+    def exchange():
+        pl.semaphore_wait(barrier, 14)
+        for n in (4, 9, 3, 8):
+            edge_copy(n).start()
+        for n in (3, 2):
+            face_copy(n).start()
+        for n in (2, 7, 1, 6, 0, 5):
+            edge_copy(n).start()
+        for n in (1, 0):
+            face_copy(n).start()
+
     left16 = left[:16]
     head16 = row[:16] < 8
 
-    def end_faces(src):
-        j0, j7 = ends(src, 1)
-        k0, k7 = ends(src, 2)
-        a = jnp.where(left16, j0[:, 0:128], pltpu.roll(k0[:, 0:128], 64, 1))
-        b = jnp.where(left16, pltpu.roll(j7[:, 384:512], 64, 1), k7[:, 384:512])
-        return jnp.where(head16, a, b)
-
-    edge_met[...] = end_faces(met) * viscosity
-    edge_vel[...] = end_faces(vel)
+    def alone():
+        for f in range(5):
+            x[f, :, 128:256] = x[f, :, 128:256] * keep
+            x[f, :, 256:384] = x[f, :, 256:384] * keep
+            low_pad[f, 8:136, :] = x[f, :, 0:128] * keep
+            high_pad[f, 8:136, :] = x[f, :, 384:512] * keep
+            above = low_pad[f, 9:137, :]
+            below = high_pad[f, 7:135, :]
+            x[f, :, 0:128] = low_pad[f, 8:136, :] + jnp.where(left, pltpu.roll(below, 64, 1), 0.0)
+            x[f, :, 384:512] = high_pad[f, 8:136, :] + jnp.where(left, 0.0, pltpu.roll(above, 64, 1))
+        for copy in later_loads:
+            copy.wait()
+        apply_operator(x, met, vel, i_tab, jk_tab, out_ref)
+
+        wide = lax.broadcasted_iota(jnp.int32, (128, 512), 1)
+        on_low = lax.rem(wide, 64) < 8
+        weight = met[1] * viscosity * vecs[0:1, :] + jnp.where(on_low, vel[1], 0.0)
+        wh, wl = halves_of(weight)
+        for cols in HALF:
+            w_ref[:, cols] = (
+                mmt(wh[:, cols], jk_tab[0, 0])
+                + mmt(wl[:, cols], jk_tab[0, 0])
+                + mmt(wh[:, cols], jk_tab[0, 1])
+            )
+
+        def low_nodes(src):
+            ah, al = halves_of(src[0])
+            bh, bl = halves_of(src[2])
+            return (
+                mm(ah, pick[:, 0:128])
+                + mm(al, pick[:, 0:128])
+                + mm(bh, pick[:, 128:256])
+                + mm(bl, pick[:, 128:256])
+            )
+
+        face_met[...] = low_nodes(met) * viscosity
+        face_vel[...] = low_nodes(vel)
+
+        edge_rows = lax.broadcasted_iota(jnp.int32, (16, 512), 0)
+        edge_wide = lax.broadcasted_iota(jnp.int32, (16, 512), 1)
+        head = edge_rows < 8
+
+        def ends(src, dim):
+            a = jnp.broadcast_to(src[dim, 0:1, :], (16, 512))
+            b = jnp.broadcast_to(src[dim, 127:128, :], (16, 512))
+            return a, b
+
+        ma, mb = ends(met, 0)
+        va, vb = ends(vel, 0)
+        ea = ma * viscosity * vecs[1:2, :] + jnp.where(edge_wide < 64, va, 0.0)
+        eb = mb * viscosity * vecs[2:3, :] + jnp.where(edge_wide >= 448, vb, 0.0)
+        eh, el = halves_of(jnp.where(head, ea, eb))
+        for cols in HALF:
+            acc = jnp.zeros((16, 256), F32)
+            for rows in HALF:
+                acc += mmt(eh[:, rows], i_tab[0, cols, rows])
+                acc += mmt(el[:, rows], i_tab[0, cols, rows])
+                acc += mmt(eh[:, rows], i_tab[1, cols, rows])
+            wi_ref[:, cols] = acc
+
+        def end_faces(src):
+            j0, j7 = ends(src, 1)
+            k0, k7 = ends(src, 2)
+            a = jnp.where(left16, j0[:, 0:128], pltpu.roll(k0[:, 0:128], 64, 1))
+            b = jnp.where(left16, pltpu.roll(j7[:, 384:512], 64, 1), k7[:, 384:512])
+            return jnp.where(head16, a, b)
+
+        edge_met[...] = end_faces(met) * viscosity
+        edge_vel[...] = end_faces(vel)
+
+    column_place = lax.rem(dom, 24)
+    early = (column_place < 2) | ((column_place == 2) & (sub == 0))
+    turn = jnp.where(early, 0, 1)
+
+    @pl.loop(0, 2)
+    def _(step):
+        pl.when(step == turn)(alone)
+        pl.when(step != turn)(exchange)
 
     def absorb(sums, block):
         route = block[320:321, :].astype(F32)
@@ -492,7 +500,7 @@
 
     sums = absorb([jnp.zeros((128, 128), F32)] * 3, send)
     for n in (0, 1, 2, 3):
-        copies[n].wait_recv()
+        face_copy(n).wait_recv()
         sums = absorb(sums, got.at[n])
     sums[2] = sums[2] + pltpu.roll(sums[2], 64, 1)
 
@@ -508,8 +516,8 @@
             + jnp.where(node < 8, pltpu.roll(below, 72, 1), 0.0)
         )
 
-    for copy in edge_copies:
-        copy.wait_recv()
+    for n in range(10):
+        edge_copy(n).wait_recv()
     tiles = [edge_got[8 * n : 8 * n + 8, :] for n in range(10)]
     high_tile = tiles[0] + tiles[1] + tiles[2] + tiles[3] + tiles[4]
     low_tile = tiles[5] + tiles[6] + tiles[7] + tiles[8] + tiles[9]
@@ -549,10 +557,10 @@
     )
     ends_ref[...] = part
 
-    for copy in copies:
-        copy.wait_send()
-    for copy in edge_copies:
-        copy.wait_send()
+    for n in range(4):
+        face_copy(n).wait_send()
+    for n in range(10):
+        edge_copy(n).wait_send()
 
 
 def finish_kernel(local, shared_ref, ends_ref, w_ref, face_met, face_vel, late, out_hbm, res, sem):

time: 29.1 us -> 26.6 us (0.914)
  Pallas kernels: 28.9 us -> 26.4 us
    pallas_call x1, Pallas kernels: 27.2 us -> 24.7 us  [shards(): pl.pallas_call(functools.partial(kernel, n_dom, n_sub), out_shape=made, i...]
where the time goes in v5:
time: 26.6 us; the launch traced here: 26.4 us
  Pallas kernels  26.4 us (99%)
    pallas_call x1, Pallas kernels, shards(): pl.pallas_call(functools.partial(kernel, n_dom, n_sub), out_shape=made, i...  24.7 us
    pallas_call x1, Pallas kernels, shards(): pl.pallas_call(finish_kernel, out_shape=jax.ShapeDtypeStruct((5, 128, 512...  1.75 us

profile of v5, /device:TPU:1, one launch (start us, length us, event | category | flops | bytes accessed | tf_op | source)
XLA Modules:
  0.0 26.4 jit_solution(11467665041429551741)
XLA Ops:
  0.0 24.7 %adjoint.1 = (f32[5,128,512]{2,1,0:T(8,128)S(1)}, f32[3,128,128]{2,1,0:T(8,128)S(1)}, f32[16,512]{1,0:T(8,128)S(1)}, f32[128,512]{1,0:T(8,128)S(1)}, f32[128,128...) custom-call(f32[5,128,512]{2,1,0:T(8,128)} %bitcast.8, f32[3,128,512]{2,1,0:T(8,128)} %bitcast.9, ...), custom_call_target="tpu_custom_call" | custom-call | tf_op jit(solution)/shard_map/adjoint/pallas_call | solution.py:620
  24.7 1.8 %finish.1 = f32[5,128,512]{2,1,0:T(8,128)} custom-call(f32[5,128,512]{2,1,0:T(8,128)S(1)} %get-tuple-element.12.local, f32[3,128,128]{2,1,0:T(8,128)S(1)} %get-tuple-element.13.shared_ref, f32[16,512]{1,0:T(8,128)S(1)} %get-tuple-element.14.ends_ref, f32[128,512]{1,0:T(8,128)S(1)} %get-tuple-element.15.w_ref, f32[128,128]{1,0:T(8,128)S(1)} %get-tuple-element.16.face_met, ...), custom_call_target="tpu_custom_call" | custom-call | tf_op jit(solution)/shard_map/finish/pallas_call | solution.py:650

commit v6 on v5

--- a/solution.py
+++ b/solution.py
@@ -226,11 +226,11 @@
     (x_hbm, met_hbm, vel_hbm, route_hbm, elem_hbm, code_hbm, hang_hbm) = refs[:7]
     (fold_hbm, i_hbm, jk_hbm, pick_hbm, late_hbm, vecs_hbm) = refs[7:13]
     (out_ref, shared_ref, ends_ref, w_ref, face_met, face_vel, late) = refs[13:20]
-    (x, met, vel, route_ref, elem_ref, code_ref, hang_ref) = refs[20:27]
-    (fold, i_tab, jk_tab, pick, vecs) = refs[27:32]
-    (send, got, edge_send, edge_got, edge_face, low_pad, high_pad, mortar_pad) = refs[32:40]
-    (wi_ref, edge_met, edge_vel) = refs[40:43]
-    (load_sem, send_sem, recv_sem, edge_send_sem, edge_recv_sem) = refs[43:48]
+    (wi_ref, edge_met, edge_vel) = refs[20:23]
+    (x, met, vel, route_ref, elem_ref, code_ref, hang_ref) = refs[23:30]
+    (fold, i_tab, jk_tab, pick, vecs) = refs[30:35]
+    (send, got, edge_send, edge_got, low_pad, high_pad, mortar_pad) = refs[35:42]
+    (load_sem, send_sem, recv_sem, edge_send_sem, edge_recv_sem) = refs[42:47]
 
     dom = lax.axis_index("dom")
     sub = lax.axis_index("sub")
@@ -280,7 +280,6 @@
     for f in range(5):
         low_pad[f, 136:144, :] = jnp.zeros((8, 128), F32)
         high_pad[f, 0:8, :] = jnp.zeros((8, 128), F32)
-    edge_face[...] = jnp.zeros((2, 8, 128), F32)
     for c in range(3):
         mortar_pad[c, 0:8, :] = jnp.zeros((8, 128), F32)
         mortar_pad[c, 136:144, :] = jnp.zeros((8, 128), F32)
@@ -392,11 +391,11 @@
 
     def exchange():
         pl.semaphore_wait(barrier, 14)
-        for n in (4, 9, 3, 8):
+        for n in (4, 3, 2, 9, 8, 7):
             edge_copy(n).start()
         for n in (3, 2):
             face_copy(n).start()
-        for n in (2, 7, 1, 6, 0, 5):
+        for n in (1, 6, 0, 5):
             edge_copy(n).start()
         for n in (1, 0):
             face_copy(n).start()
@@ -483,25 +482,30 @@
         pl.when(step == turn)(alone)
         pl.when(step != turn)(exchange)
 
-    def absorb(sums, block):
-        route = block[320:321, :].astype(F32)
-        elem = block[321:322, :].astype(F32)
-        dest = jnp.where(route == dom.astype(F32), elem, -1.0)
-        hit = (jnp.broadcast_to(dest, (128, 128)) == row.astype(F32)).astype(F32).astype(BF)
-        tail = block[256:320, :].astype(F32)
-        last = jnp.concatenate(
-            [jnp.where(left[:64], tail, 0.0), jnp.where(left[:64], 0.0, tail)], axis=0
-        ).astype(BF)
+    def absorb(sums, blocks):
+        hits, firsts, seconds, lasts = [], [], [], []
+        for block in blocks:
+            route = block[320:321, :].astype(F32)
+            elem = block[321:322, :].astype(F32)
+            dest = jnp.where(route == dom.astype(F32), elem, -1.0)
+            hit = jnp.broadcast_to(dest, (128, 128)) == row.astype(F32)
+            hits.append(hit.astype(F32).astype(BF))
+            tail = block[256:320, :].astype(F32)
+            firsts.append(block[0:128, :])
+            seconds.append(block[128:256, :])
+            lasts += [jnp.where(left[:64], tail, 0.0), jnp.where(left[:64], 0.0, tail)]
+        hits = jnp.concatenate(hits, axis=1)
         return [
-            sums[0] + mm(hit, block[0:128, :]),
-            sums[1] + mm(hit, block[128:256, :]),
-            sums[2] + mm(hit, last),
+            sums[0] + mm(hits, jnp.concatenate(firsts, axis=0)),
+            sums[1] + mm(hits, jnp.concatenate(seconds, axis=0)),
+            sums[2] + mm(hits, jnp.concatenate(lasts, axis=0).astype(BF)),
         ]
 
-    sums = absorb([jnp.zeros((128, 128), F32)] * 3, send)
-    for n in (0, 1, 2, 3):
-        face_copy(n).wait_recv()
-        sums = absorb(sums, got.at[n])
+    sums = absorb([jnp.zeros((128, 128), F32)] * 3, [send])
+    for pair in ((0, 1), (2, 3)):
+        for n in pair:
+            face_copy(n).wait_recv()
+        sums = absorb(sums, [got.at[n] for n in pair])
     sums[2] = sums[2] + pltpu.roll(sums[2], 64, 1)
 
     node = lax.rem(lane, 64)
@@ -521,6 +525,24 @@
     tiles = [edge_got[8 * n : 8 * n + 8, :] for n in range(10)]
     high_tile = tiles[0] + tiles[1] + tiles[2] + tiles[3] + tiles[4]
     low_tile = tiles[5] + tiles[6] + tiles[7] + tiles[8] + tiles[9]
+    ends_ref[0:8, :] = high_tile * jnp.where(place > 0, 1.0, 0.0)
+    ends_ref[8:16, :] = low_tile * jnp.where(place < total - 1, 1.0, 0.0)
+
+    for n in range(4):
+        face_copy(n).wait_send()
+    for n in range(10):
+        edge_copy(n).wait_send()
+
+
+def finish_kernel(*refs):
+    (local, shared_ref, ends_ref, w_ref, face_met, face_vel, late) = refs[:7]
+    (wi_ref, edge_met, edge_vel, out_hbm, res, edge_face, sem) = refs[7:]
+    left = lax.broadcasted_iota(jnp.int32, (128, 128), 1) < 64
+    lane = lax.broadcasted_iota(jnp.int32, (128, 128), 1)
+    left16 = left[:16]
+    head16 = lax.broadcasted_iota(jnp.int32, (16, 128), 0) < 8
+    edge_face[...] = jnp.zeros((2, 8, 128), F32)
+    high_tile, low_tile = ends_ref[0:8, :], ends_ref[8:16, :]
     lane8 = lane[:8]
     at_high = (lane8 >= 64) & (lane8 < 72)
     at_low = lane8 < 8
@@ -530,10 +552,8 @@
         c, g = divmod(f, 2)
         edge_face[0, f : f + 1, :] = high_tile[3 + f : 4 + f, :] + highs[g][c : c + 1, :]
         edge_face[1, f : f + 1, :] = low_tile[3 + f : 4 + f, :] + lows[g][c : c + 1, :]
-    has_next = jnp.where(place < total - 1, 1.0, 0.0)
-    has_prev = jnp.where(place > 0, 1.0, 0.0)
-    from_prev = edge_face[0] * has_prev
-    from_next = edge_face[1] * has_next
+    from_prev = edge_face[0]
+    from_next = edge_face[1]
     face = jnp.concatenate(
         [
             jnp.where(left[:8], pltpu.roll(from_prev, 64, 1), from_prev),
@@ -555,18 +575,8 @@
         ],
         axis=1,
     )
-    ends_ref[...] = part
-
-    for n in range(4):
-        face_copy(n).wait_send()
-    for n in range(10):
-        edge_copy(n).wait_send()
-
-
-def finish_kernel(local, shared_ref, ends_ref, w_ref, face_met, face_vel, late, out_hbm, res, sem):
-    left = lax.broadcasted_iota(jnp.int32, (128, 128), 1) < 64
     shared = [shared_ref[c] for c in range(3)]
-    pairs = jnp.concatenate([side_by_side(part) for part in shared], axis=0)
+    pairs = jnp.concatenate([side_by_side(one) for one in shared], axis=0)
     slopes = mm(pairs, late[:, FORWARD : FORWARD + 256]) + mm(
         pairs, late[:, FORWARD + 256 : FORWARD + 512]
     )
@@ -593,8 +603,8 @@
             spread = every[n][g][128 * c : 128 * c + 128]
             low = lows[n][128 * f : 128 * f + 128]
             res[f, :, cols] = local[f, :, cols] + spread * w_ref[:, cols] + low
-        res[f, 0:1, :] = res[f, 0:1, :] + ends_ref[f : f + 1, :]
-        res[f, 127:128, :] = res[f, 127:128, :] + ends_ref[8 + f : 9 + f, :]
+        res[f, 0:1, :] = res[f, 0:1, :] + part[f : f + 1, :]
+        res[f, 127:128, :] = res[f, 127:128, :] + part[8 + f : 9 + f, :]
         copy = pltpu.make_async_copy(res.at[f], out_hbm.at[f], sem.at[f])
         copy.start()
         copies.append(copy)
@@ -610,11 +620,14 @@
     made = [
         pltpu.VMEM((5, 128, 512), F32),
         pltpu.VMEM((3, 128, 128), F32),
-        pltpu.VMEM((16, 512), F32),
+        pltpu.VMEM((16, 128), F32),
         pltpu.VMEM((128, 512), F32),
         pltpu.VMEM((128, 128), F32),
         pltpu.VMEM((128, 128), F32),
         pltpu.VMEM(consts[4].shape, BF),
+        pltpu.VMEM((16, 512), F32),
+        pltpu.VMEM((16, 128), F32),
+        pltpu.VMEM((16, 128), F32),
     ]
     held = fields + rows + consts[:4] + consts[5:]
     handed = pl.pallas_call(
@@ -628,13 +641,9 @@
             pltpu.VMEM((4, ROWS, 128), BF),
             pltpu.VMEM((80, 128), F32),
             pltpu.VMEM((80, 128), F32),
-            pltpu.VMEM((2, 8, 128), F32),
             pltpu.VMEM((5, 144, 128), F32),
             pltpu.VMEM((5, 144, 128), F32),
             pltpu.VMEM((3, 144, 128), F32),
-            pltpu.VMEM((16, 512), F32),
-            pltpu.VMEM((16, 128), F32),
-            pltpu.VMEM((16, 128), F32),
             pltpu.SemaphoreType.DMA((17,)),
             pltpu.SemaphoreType.DMA((4,)),
             pltpu.SemaphoreType.DMA((4,)),
@@ -652,7 +661,11 @@
         out_shape=jax.ShapeDtypeStruct((5, 128, 512), F32),
         in_specs=[pl.BlockSpec(memory_space=pltpu.VMEM)] * len(handed),
         out_specs=pl.BlockSpec(memory_space=pltpu.HBM),
-        scratch_shapes=[pltpu.VMEM((5, 128, 512), F32), pltpu.SemaphoreType.DMA((5,))],
+        scratch_shapes=[
+            pltpu.VMEM((5, 128, 512), F32),
+            pltpu.VMEM((2, 8, 128), F32),
+            pltpu.SemaphoreType.DMA((5,)),
+        ],
         compiler_params=pltpu.CompilerParams(vmem_limit_bytes=32 << 20),
         name="finish",
     )(*handed)

time: 26.6 us -> 26.7 us (level)
    pallas_call x1, Pallas kernels: 1.75 us -> 2.18 us  [shards(): pl.pallas_call(finish_kernel, out_shape=jax.ShapeDtypeStruct((5, 128, 512...]
    pallas_call x1, Pallas kernels: 24.7 us -> 24.4 us  [shards(): pl.pallas_call(functools.partial(kernel, n_dom, n_sub), out_shape=made, i...]
where the time goes in v6:
time: 26.7 us; the launch traced here: 26.6 us
  Pallas kernels  26.6 us (100%)
    pallas_call x1, Pallas kernels, shards(): pl.pallas_call(functools.partial(kernel, n_dom, n_sub), out_shape=made, i...  24.4 us
    pallas_call x1, Pallas kernels, shards(): pl.pallas_call(finish_kernel, out_shape=jax.ShapeDtypeStruct((5, 128, 512...  2.18 us

profile of v6, /device:TPU:1, one launch (start us, length us, event | category | flops | bytes accessed | tf_op | source)
XLA Modules:
  0.0 26.6 jit_solution(9346709440744759831)
XLA Ops:
  0.0 24.4 %adjoint.1 = (f32[5,128,512]{2,1,0:T(8,128)S(1)}, f32[3,128,128]{2,1,0:T(8,128)S(1)}, f32[16,128]{1,0:T(8,128)S(1)}, f32[128,512]{1,0:T(8,128)S(1)}, f32[128,128...) custom-call(f32[5,128,512]{2,1,0:T(8,128)} %bitcast.8, ...), custom_call_target="tpu_custom_call" | custom-call | tf_op jit(solution)/shard_map/adjoint/pallas_call | solution.py:633
  24.4 2.2 %finish.1 = f32[5,128,512]{2,1,0:T(8,128)} custom-call(f32[5,128,512]{2,1,0:T(8,128)S(1)} %get-tuple-element.15.refs_0_, f32[3,128,128]{2,1,0:T(8,128)S(1)} %get-tuple-element.16.refs_1_, f32[16,128]{1,0:T(8,128)S(1)} %get-tuple-element.17.refs_2_, f32[128,512]{1,0:T(8,128)S(1)} %get-tuple-element.18.refs_3_, f32[128,128]{1,0:T(8,128)S(1)} %get-tuple-element.19.refs_4_, ...), custom_call_target="tpu_custom_call" | custom-call | tf_op jit(solution)/shard_map/finish/pallas_call | solution.py:659

commit v7 on v5

--- a/solution.py
+++ b/solution.py
@@ -222,15 +222,46 @@
         out_ref[:, :, cols] = total.reshape(5, 128, 256)
 
 
+def finish(res, shared_ref, w_ref, face_met, face_vel, late):
+    left = lax.broadcasted_iota(jnp.int32, (128, 128), 1) < 64
+    shared = [shared_ref[c] for c in range(3)]
+    pairs = jnp.concatenate([side_by_side(part) for part in shared], axis=0)
+    slopes = mm(pairs, late[:, FORWARD : FORWARD + 256]) + mm(
+        pairs, late[:, FORWARD + 256 : FORWARD + 512]
+    )
+    inners = []
+    for f in range(5):
+        c, g = divmod(f, 2)
+        twice = jnp.where(left == (g == 0), shared[c], pltpu.roll(shared[c], 64, 1))
+        slope = slopes[128 * c : 128 * c + 128, 128 * g : 128 * g + 128]
+        inners.append(side_by_side(face_met[...] * slope + face_vel[...] * twice))
+    inners = jnp.concatenate(inners, axis=0)
+    every, lows = [], []
+    for at in (0, 256):
+        even = mm(pairs, late[:, EXPAND + at : EXPAND + at + 256])
+        odd = mm(pairs[:256], late[:, EXPAND + 512 + at : EXPAND + 512 + at + 256])
+        every.append((even, odd))
+        lows.append(
+            mm(inners, late[:, DOWN + at : DOWN + at + 256])
+            + mm(inners, late[:, DOWN + 512 + at : DOWN + 512 + at + 256])
+        )
+    for f in range(5):
+        c, g = divmod(f, 2)
+        for n, cols in enumerate(HALF):
+            spread = every[n][g][128 * c : 128 * c + 128]
+            low = lows[n][128 * f : 128 * f + 128]
+            res[f, :, cols] = res[f, :, cols] + spread * w_ref[:, cols] + low
+
+
 def kernel(n_dom, n_sub, *refs):
     (x_hbm, met_hbm, vel_hbm, route_hbm, elem_hbm, code_hbm, hang_hbm) = refs[:7]
     (fold_hbm, i_hbm, jk_hbm, pick_hbm, late_hbm, vecs_hbm) = refs[7:13]
-    (out_ref, shared_ref, ends_ref, w_ref, face_met, face_vel, late) = refs[13:20]
-    (x, met, vel, route_ref, elem_ref, code_ref, hang_ref) = refs[20:27]
-    (fold, i_tab, jk_tab, pick, vecs) = refs[27:32]
-    (send, got, edge_send, edge_got, edge_face, low_pad, high_pad, mortar_pad) = refs[32:40]
-    (wi_ref, edge_met, edge_vel) = refs[40:43]
-    (load_sem, send_sem, recv_sem, edge_send_sem, edge_recv_sem) = refs[43:48]
+    (out_ref, shared_ref, w_ref, face_met, face_vel, late) = refs[13:19]
+    (x, met, vel, route_ref, elem_ref, code_ref, hang_ref) = refs[19:26]
+    (fold, i_tab, jk_tab, pick, vecs) = refs[26:31]
+    (send, got, edge_send, edge_got, edge_face, low_pad, high_pad, mortar_pad) = refs[31:39]
+    (wi_ref, edge_met, edge_vel) = refs[39:42]
+    (load_sem, send_sem, recv_sem, edge_send_sem, edge_recv_sem) = refs[42:47]
 
     dom = lax.axis_index("dom")
     sub = lax.axis_index("sub")
@@ -516,6 +547,8 @@
             + jnp.where(node < 8, pltpu.roll(below, 72, 1), 0.0)
         )
 
+    finish(out_ref, shared_ref, w_ref, face_met, face_vel, late)
+
     for n in range(10):
         edge_copy(n).wait_recv()
     tiles = [edge_got[8 * n : 8 * n + 8, :] for n in range(10)]
@@ -555,51 +588,14 @@
         ],
         axis=1,
     )
-    ends_ref[...] = part
+    for f in range(5):
+        out_ref[f, 0:1, :] = out_ref[f, 0:1, :] + part[f : f + 1, :]
+        out_ref[f, 127:128, :] = out_ref[f, 127:128, :] + part[8 + f : 9 + f, :]
 
     for n in range(4):
         face_copy(n).wait_send()
     for n in range(10):
         edge_copy(n).wait_send()
-
-
-def finish_kernel(local, shared_ref, ends_ref, w_ref, face_met, face_vel, late, out_hbm, res, sem):
-    left = lax.broadcasted_iota(jnp.int32, (128, 128), 1) < 64
-    shared = [shared_ref[c] for c in range(3)]
-    pairs = jnp.concatenate([side_by_side(part) for part in shared], axis=0)
-    slopes = mm(pairs, late[:, FORWARD : FORWARD + 256]) + mm(
-        pairs, late[:, FORWARD + 256 : FORWARD + 512]
-    )
-    inners = []
-    for f in range(5):
-        c, g = divmod(f, 2)
-        twice = jnp.where(left == (g == 0), shared[c], pltpu.roll(shared[c], 64, 1))
-        slope = slopes[128 * c : 128 * c + 128, 128 * g : 128 * g + 128]
-        inners.append(side_by_side(face_met[...] * slope + face_vel[...] * twice))
-    inners = jnp.concatenate(inners, axis=0)
-    every, lows = [], []
-    for at in (0, 256):
-        even = mm(pairs, late[:, EXPAND + at : EXPAND + at + 256])
-        odd = mm(pairs[:256], late[:, EXPAND + 512 + at : EXPAND + 512 + at + 256])
-        every.append((even, odd))
-        lows.append(
-            mm(inners, late[:, DOWN + at : DOWN + at + 256])
-            + mm(inners, late[:, DOWN + 512 + at : DOWN + 512 + at + 256])
-        )
-    copies = []
-    for f in range(5):
-        c, g = divmod(f, 2)
-        for n, cols in enumerate(HALF):
-            spread = every[n][g][128 * c : 128 * c + 128]
-            low = lows[n][128 * f : 128 * f + 128]
-            res[f, :, cols] = local[f, :, cols] + spread * w_ref[:, cols] + low
-        res[f, 0:1, :] = res[f, 0:1, :] + ends_ref[f : f + 1, :]
-        res[f, 127:128, :] = res[f, 127:128, :] + ends_ref[8 + f : 9 + f, :]
-        copy = pltpu.make_async_copy(res.at[f], out_hbm.at[f], sem.at[f])
-        copy.start()
-        copies.append(copy)
-    for copy in copies:
-        copy.wait()
 
 
 def shards(n_dom, n_sub, adjoint_field, metric, velocity, route, element, code, hanging):
@@ -608,21 +604,19 @@
     consts = [jnp.asarray(t) for t in tables()]
     operands = [pltpu.with_memory_space_constraint(a, pltpu.HBM) for a in fields + rows + consts]
     made = [
-        pltpu.VMEM((5, 128, 512), F32),
         pltpu.VMEM((3, 128, 128), F32),
-        pltpu.VMEM((16, 512), F32),
         pltpu.VMEM((128, 512), F32),
         pltpu.VMEM((128, 128), F32),
         pltpu.VMEM((128, 128), F32),
         pltpu.VMEM(consts[4].shape, BF),
     ]
     held = fields + rows + consts[:4] + consts[5:]
-    handed = pl.pallas_call(
+    result = pl.pallas_call(
         functools.partial(kernel, n_dom, n_sub),
-        out_shape=made,
+        out_shape=pltpu.VMEM((5, 128, 512), F32),
         in_specs=[pl.BlockSpec(memory_space=pltpu.HBM)] * len(operands),
-        out_specs=[pl.BlockSpec(memory_space=pltpu.VMEM)] * len(made),
-        scratch_shapes=[pltpu.VMEM(a.shape, a.dtype) for a in held]
+        out_specs=pl.BlockSpec(memory_space=pltpu.VMEM),
+        scratch_shapes=made + [pltpu.VMEM(a.shape, a.dtype) for a in held]
         + [
             pltpu.VMEM((ROWS, 128), BF),
             pltpu.VMEM((4, ROWS, 128), BF),
@@ -646,16 +640,6 @@
         ),
         name="adjoint",
     )(*operands)
-    handed = [pltpu.with_memory_space_constraint(a, pltpu.VMEM) for a in handed]
-    result = pl.pallas_call(
-        finish_kernel,
-        out_shape=jax.ShapeDtypeStruct((5, 128, 512), F32),
-        in_specs=[pl.BlockSpec(memory_space=pltpu.VMEM)] * len(handed),
-        out_specs=pl.BlockSpec(memory_space=pltpu.HBM),
-        scratch_shapes=[pltpu.VMEM((5, 128, 512), F32), pltpu.SemaphoreType.DMA((5,))],
-        compiler_params=pltpu.CompilerParams(vmem_limit_bytes=32 << 20),
-        name="finish",
-    )(*handed)
     return jnp.transpose(result, (1, 0, 2))
 
 

time: 26.6 us -> 26.6 us (level)
  local copies, waits for them, and re-layouts: 0 us -> 1.06 us
  Pallas kernels: 26.4 us -> 25.4 us
    unnamed x0 -> x1, local copies, waits for them, and re-layouts: none -> 1.06 us
    pallas_call x2 -> x1, Pallas kernels: 26.4 us -> 25.4 us  [shards(): pl.pallas_call(functools.partial(kernel, n_dom, n_sub), out_shape=pltpu.V...]
where the time goes in v7:
time: 26.6 us; the launch traced here: 26.4 us
  Pallas kernels  25.4 us (95%)
  local copies, waits for them, and re-layouts  1.06 us (4%)
    pallas_call x1, Pallas kernels, shards(): pl.pallas_call(functools.partial(kernel, n_dom, n_sub), out_shape=pltpu.V...  25.4 us
    unnamed x1, local copies, waits for them, and re-layouts  1.06 us

profile of v7, /device:TPU:1, one launch (start us, length us, event | category | flops | bytes accessed | tf_op | source)
XLA Modules:
  0.0 26.4 jit_solution(7227192578767696653)
XLA Ops:
  0.0 25.4 %adjoint.1 = f32[5,128,512]{2,1,0:T(8,128)S(1)} custom-call(f32[5,128,512]{2,1,0:T(8,128)} %bitcast.9, f32[3,128,512]{2,1,0:T(8,128)} %bitcast.10, f32[3,128,512]{2,1,0:T(8,128)} %bitcast.11, s32[1,128]{1,0:T(1,128)} %bitcast.12, s32[1,128]{1,0:T(1,128)} %bitcast.13, s32[1,128]{1,0:T(1,128)} %bitcast.14, s32[1,128]{1,0:T(1,128)} %bitcast.15, ...), custom_call_target="tpu_custom_call" | custom-call | tf_op jit(solution)/shard_map/adjoint/pallas_call | solution.py:614
  25.4 1.1 %copy.15 = f32[128,5,512]{2,0,1:T(8,128)} copy(f32[128,5,512]{2,0,1:T(8,128)S(1)} %bitcast.8) | data formatting | bytes 2621440
